TPU v7x, 32 devices: a whole 2x2x4 slice. The times are simulated.
32 devices in a mesh: prow: 8 (over y, x, core), pcol: 4 (over z).
Axes of the slice: x: 2, y: 2, z: 4, core: 2. Of those that a mesh axis runs over, the one named last changes fastest.
Arguments:
- inverse_trailing: bfloat16 [18432, 18432], P('prow', 'pcol'), may hold values from -6 to 6
- panel: bfloat16 [18432, 256], P('prow'), may hold values from -0.0625 to 0.0625
- supernode_inverse: float32 [256, 256], replicated, may hold values from -6 to 6
- block_live: int32 [72], replicated, may hold values from 0 to 1, as said below
Outputs:
- column_inverse: float32 [18432, 256], P('prow')
- diagonal_inverse: float32 [256, 256], replicated
Inputs may be any that keep to these rules, and one draw needn't show every extreme that they name: Each aligned group of 9 consecutive block rows (the rows of one index of prow) holds at least one block row with block_live 1.
All inputs are finite; a program needn't handle non-finite values.
Results may differ from a plain program's by a relative error of at most 0.0003.
Values may be sent and summed in bfloat16 or wider, within the bound.
No kernel may reach another device: no remote copies, remote signals or barrier semaphores. Data moves between devices by JAX's collectives and lax.ppermute only.
A program may use at most 128 MiB of HBM per device.

v0:
```python
import functools

import jax
import jax.numpy as jnp
from jax import lax
from jax.experimental import pallas as pl
from jax.experimental.pallas import tpu as pltpu
from jax.sharding import PartitionSpec as P


AXES = ("prow", "pcol")
SMALLEST = 9
SCRATCH = 8 << 20
ROWS = 64
TAIL = 16
STEPS = 64.0
TOP = 32760.0
LN2 = 0.6931471805599453
F32 = jnp.float32
VMEM = pl.BlockSpec(memory_space=pltpu.VMEM)
SMEM = pl.BlockSpec(memory_space=pltpu.SMEM)
HBM = pl.BlockSpec(memory_space=pltpu.HBM)


def near(x):
    return pltpu.with_memory_space_constraint(x, pltpu.VMEM)


def kernel(body, outs, specs, out_specs, **options):
    params = pltpu.CompilerParams(vmem_limit_bytes=SCRATCH)
    return pl.pallas_call(
        body, out_shape=outs, in_specs=specs, out_specs=out_specs, compiler_params=params, **options
    )


def step_of(top):
    return jnp.ceil(jnp.log(jnp.maximum(top, 1e-30)) * (STEPS / LN2))


def top_of(step):
    return jnp.exp(step * (LN2 / STEPS))


def to_ints(x, step):
    return jnp.round(x * (jnp.exp(step * (-LN2 / STEPS)) * TOP)).astype(jnp.int32).astype(jnp.int16)


def to_floats(q, step):
    return q.astype(jnp.int32).astype(F32) * (top_of(step) * (1.0 / TOP))


def read_steps(message):
    return message[message.shape[0] - TAIL :, :].astype(jnp.int32).astype(F32)


def write_steps(message, steps):
    message[message.shape[0] - TAIL :, :] = steps.astype(jnp.int32).astype(jnp.int16)


def by_rows(size, work):
    def one(r, _):
        work(r)
        return 0

    lax.fori_loop(0, size // ROWS, one, 0)


def rows_at(block, r, size):
    return pl.ds(pl.multiple_of(block * size + r * ROWS, ROWS), ROWS)


def store_message(message, part, size):
    count = part.shape[0] // size
    steps = []
    for i in range(count):
        top = jnp.max(jnp.abs(part[i * size : (i + 1) * size, :]), axis=0, keepdims=True)
        steps.append(step_of(top))

        def one(r, i=i):
            at = rows_at(i, r, size)
            message[at, :] = to_ints(part[at, :], steps[i])

        by_rows(size, one)
    pad = jnp.zeros((TAIL - count, message.shape[1]), F32)
    write_steps(message, jnp.concatenate(steps + [pad], axis=0))


def is_middle(n_pcol):
    pcol = lax.axis_index("pcol")
    return jnp.logical_or(pcol == n_pcol // 2 - 1, pcol == n_pcol // 2)


def pack_kernel(live, panel, *refs, ranges, n, per, ratio):
    packs, (rows, cols, valid, sem) = refs[:-4], refs[-4:]
    size = panel.shape[0] // per
    prow, pcol = lax.axis_index("prow"), lax.axis_index("pcol")
    core = prow % ratio

    def each_copy(act):
        slot = 0
        for k in range(per):
            alive = live[prow * per + k] != 0
            for (first, last), pack in zip(ranges, packs):
                inside = jnp.logical_and(slot >= first, slot < last)

                @pl.when(jnp.logical_and(alive, inside))
                def _():
                    start = pl.multiple_of((slot - first) * size, size)
                    act(
                        pltpu.make_async_copy(
                            panel.at[pl.ds(k * size, size), :], pack.at[pl.ds(start, size), :], sem
                        )
                    )

            slot = slot + alive.astype(jnp.int32)
        return slot

    count = each_copy(lambda copy: copy.start())
    for i in range(n):
        rows[i] = 0
        valid[i] = (count > i).astype(jnp.int32)
        cols[i] = 0
        cols[n + i] = 0
        for (first, last), pack in zip(ranges, packs):
            if first <= i < last:

                @pl.when(count <= i)
                def _():
                    at = slice((i - first) * size, (i - first + 1) * size)
                    pack[at, :] = jnp.zeros((size, pack.shape[1]), pack.dtype)

    slot = 0
    for k in range(per):
        alive = live[prow * per + k] != 0

        @pl.when(alive)
        def _():
            rows[slot] = k

        slot = slot + alive.astype(jnp.int32)
    for side in range(ratio):
        which = core if side == 0 else ratio - 1 - core
        slot = 0
        for k in range(per):
            alive = live[(pcol * ratio + which) * per + k] != 0

            @pl.when(alive)
            def _():
                cols[side * n + slot] = which * per + k

            slot = slot + alive.astype(jnp.int32)
    each_copy(lambda copy: copy.wait())


def fetch_kernel(rows, cols, a, out, sem, *, first, size):
    for i in range(out.shape[0] // size):
        r = pl.multiple_of(rows[first + i] * size, size)

        def copy(j, _, i=i, r=r):
            c = pl.multiple_of(cols[j] * size, size)
            to = out.at[pl.ds(i * size, size), pl.ds(pl.multiple_of(j * size, size), size)]
            pltpu.make_async_copy(a.at[pl.ds(r, size), pl.ds(c, size)], to, sem).start()
            return 0

        lax.fori_loop(0, out.shape[1] // size, copy, 0)
    whole = a.at[pl.ds(0, out.shape[0]), pl.ds(0, out.shape[1])]
    pltpu.make_async_copy(whole, out, sem).wait()


def merge_kernel(a, b, xa1, xa2, da1, da2, ya, yb1, yb2, db1, db2, xb, full, *, ratio):
    root = lax.axis_index("prow") // ratio == lax.axis_index("pcol")

    @pl.when(root)
    def _():
        full[: a.shape[0], :] = a[...]
        full[a.shape[0] :, :] = b[...]

    @pl.when(jnp.logical_not(root))
    def _():
        start = 0
        for whole, early, late in ((ya, (xa1, xa2), (da1, da2)), (xb, (yb1, yb2), (db1, db2))):
            inner = 0
            for e, l in zip(early, late):
                size = e.shape[0]
                full[start : start + size, :] = whole[inner : inner + size, :] + e[...] + l[...]
                start += size
                inner += size


def product_kernel(left, own, other, a, b, *refs, first, size):
    part, message, term = refs[-3:]
    n_rows = own.shape[0]
    acc = jnp.dot(left[:, :n_rows], own[...], preferred_element_type=F32)
    part[...] = acc + jnp.dot(left[:, n_rows:], other[...], preferred_element_type=F32)
    store_message(message, part, size)
    contract = (((0,), (0,)), ((), ()))
    total = refs[0][...] if len(refs) == 4 else None
    split = a.shape[0] // size
    for i in range(left.shape[0] // size):
        at = first + i
        local = a[at * size : (at + 1) * size, :] if at < split else b[(at - split) * size : (at - split + 1) * size, :]
        x = part[i * size : (i + 1) * size, :]
        high = x.astype(jnp.bfloat16)
        low = (x - high.astype(F32)).astype(jnp.bfloat16)
        for y in (high, low):
            piece = lax.dot_general(local, y, contract, preferred_element_type=F32)
            total = piece if total is None else total + piece
    term[...] = total


def join_kernel(part, mine, came, message, *, size):
    before, arrived = read_steps(mine), read_steps(came)
    steps = step_of(top_of(before) + top_of(arrived))
    write_steps(message, steps)
    for i in range(part.shape[0] // size):

        def one(r, i=i):
            at = rows_at(i, r, size)
            message[at, :] = to_ints(part[at, :] + to_floats(came[at, :], arrived[i : i + 1, :]), steps[i : i + 1, :])

        by_rows(size, one)


def meet_kernel(mine, came, message, *, size, n_pcol):
    low_side = lax.axis_index("pcol") < n_pcol // 2
    a, b = read_steps(mine), read_steps(came)
    steps = step_of(top_of(a) + top_of(b))
    write_steps(message, steps)
    first, second = jnp.where(low_side, a, b), jnp.where(low_side, b, a)
    for i in range((mine.shape[0] - TAIL) // size):

        def one(r, i=i):
            at = rows_at(i, r, size)
            x, y = mine[at, :], came[at, :]
            u, v = jnp.where(low_side, x, y), jnp.where(low_side, y, x)
            total = to_floats(u, first[i : i + 1, :]) + to_floats(v, second[i : i + 1, :])
            message[at, :] = to_ints(total, steps[i : i + 1, :])

        by_rows(size, one)


def spread_kernel(rows, valid, live, total, came, *refs, first, size, per, n_pcol, fill):
    out, blocks, zeros, sem = refs[-4:]
    middle = is_middle(n_pcol)
    count = blocks.shape[0] // size
    prow = lax.axis_index("prow")

    def zero(k):
        return pltpu.make_async_copy(zeros, out.at[pl.ds(k * size, size), :], sem.at[count + k])

    def copy(i):
        start = pl.multiple_of(rows[first + i] * size, size)
        return pltpu.make_async_copy(blocks.at[pl.ds(i * size, size), :], out.at[pl.ds(start, size), :], sem.at[i])

    if fill:
        zeros[...] = jnp.zeros_like(zeros)
        for k in range(per):
            pl.when(live[prow * per + k] == 0)(lambda k=k: zero(k).start())
    steps = jnp.where(middle, read_steps(total), read_steps(came))
    for i in range(count):

        def one(r, i=i):
            at = rows_at(i, r, size)
            blocks[at, :] = -to_floats(jnp.where(middle, total[at, :], came[at, :]), steps[i : i + 1, :])

        by_rows(size, one)
        pl.when(valid[first + i] != 0)(lambda i=i: copy(i).start())
    for i in range(count):
        pl.when(valid[first + i] != 0)(lambda i=i: copy(i).wait())
    if fill:
        for k in range(per):
            pl.when(live[prow * per + k] == 0)(lambda k=k: zero(k).wait())


def pick_kernel(total, came, out, *, n_pcol):
    out[...] = jnp.where(is_middle(n_pcol), total[...], came[...])


def add_kernel(x, y, out):
    out[...] = x[...] + y[...]


def halves_kernel(term, keep, give, *, ratio):
    core = lax.axis_index("prow") % ratio
    half = keep.shape[1]
    left, right = term[:, :half], term[:, half:]
    keep[...] = jnp.where(core == 0, left, right)
    give[...] = jnp.where(core == 0, right, left)


def root_kernel(a, b, out, *, ratio):
    root = lax.axis_index("prow") // ratio == lax.axis_index("pcol")
    top = a.shape[0]
    out[:top, :] = jnp.where(root, a[...], jnp.zeros_like(a))
    out[top:, :] = jnp.where(root, b[...], jnp.zeros_like(b))


def diagonal_kernel(base, mine, other, out, *, ratio):
    core = lax.axis_index("prow") % ratio
    half = out.shape[1] // ratio
    size = out.shape[0]
    left = jnp.where(core == 0, mine[...], other[...])
    right = jnp.where(core == 0, other[...], mine[...])
    for h, m in ((0, left), (1, right)):
        value = to_floats(m[:size, :], m[size : size + 1, :].astype(jnp.int32).astype(F32))
        out[:, h * half : (h + 1) * half] = base[:, h * half : (h + 1) * half] + value


def chunk_sizes(n):
    return {9: (3, 3, 2, 1), 8: (3, 2, 2, 1), 7: (3, 2, 1, 1), 6: (2, 2, 1, 1), 5: (2, 2, 1)}.get(n, (n,))


def packed_step(inverse_trailing, panel, supernode_inverse, block_live, *, n, n_prow, n_pcol):
    rows_dev, width = panel.shape
    per = block_live.shape[0] // n_prow
    size = rows_dev // per
    ratio = n_prow // n_pcol
    chips = n_prow // ratio

    def send(value, target):
        pairs = []
        for p in range(n_prow):
            for c in range(n_pcol):
                to = target(p, c)
                if to is not None:
                    pairs.append((p * n_pcol + c, to[0] * n_pcol + to[1]))
        return near(lax.ppermute(value, AXES, pairs))

    def place(p, c):
        return (p // ratio) ^ c

    inverse_trailing = pltpu.with_memory_space_constraint(inverse_trailing, pltpu.HBM)

    panel = pltpu.with_memory_space_constraint(panel, pltpu.HBM)

    split = n - n // 2
    cuts = (0, split - split // 2, split, n - (n - split) // 2, n)
    ranges = [(0, split), (split, n)] + list(zip(cuts[:-1], cuts[1:]))
    tables = [jax.ShapeDtypeStruct((k,), jnp.int32) for k in (n, 2 * n, n)]
    a, b, a1, a2, b1, b2, rows, cols, valid = kernel(
        functools.partial(pack_kernel, ranges=ranges, n=n, per=per, ratio=ratio),
        [pltpu.VMEM(((q - p) * size, width), panel.dtype) for p, q in ranges] + tables,
        [SMEM, HBM], [VMEM] * len(ranges) + [SMEM] * 3,
        scratch_shapes=[pltpu.SemaphoreType.DMA],
    )(block_live, panel)

    def to_x(p, c):
        return (p ^ ratio, c)

    def to_y(p, c):
        return (p ^ (2 * ratio), c)

    def only(step, *places):
        return lambda p, c: step(p, c) if place(p, c) in places else None

    chunks = chunk_sizes(n)
    lefts = []
    first = 0
    for count in chunks:
        lefts.append(
            kernel(
                functools.partial(fetch_kernel, first=first, size=size),
                pltpu.VMEM((count * size, 2 * n * size), inverse_trailing.dtype), [SMEM, SMEM, HBM], VMEM,
                scratch_shapes=[pltpu.SemaphoreType.DMA],
            )(rows, cols, inverse_trailing)
        )
        first += count
    if chips == 4:
        xa1 = send(a1, only(to_x, 0))
        yb1 = send(b1, only(to_y, 0))
        xa2 = send(a2, only(to_x, 0))
        yb2 = send(b2, only(to_y, 0))
        xb = send(b, only(to_x, 0))
        ya = send(a, only(to_y, 0))
        da1 = send(xa1, only(to_y, 1))
        db1 = send(yb1, only(to_x, 2))
        da2 = send(xa2, only(to_y, 1))
        db2 = send(yb2, only(to_x, 2))
        own = kernel(
            functools.partial(merge_kernel, ratio=ratio),
            pltpu.VMEM((n * size, width), panel.dtype), [VMEM] * 12, VMEM,
        )(a, b, xa1, xa2, da1, da2, ya, yb1, yb2, db1, db2, xb)
    else:
        shape = pltpu.VMEM((n * size, width), panel.dtype)
        own = kernel(functools.partial(root_kernel, ratio=ratio), shape, [VMEM] * 2, VMEM)(a, b)
        bit = 1
        while bit < chips:
            def spread(p, c, bit=bit):
                return (p ^ (bit * ratio), c) if place(p, c) < bit else None

            own = kernel(add_kernel, shape, [VMEM] * 2, VMEM)(own, send(own, spread))
            bit *= 2
    swap = lambda p, c: (p ^ 1, c)
    other = send(own, swap)

    middle = n_pcol // 2

    def sum_over_line(part, message):
        out = pltpu.VMEM(message.shape, jnp.int16)
        mine = message
        for hop in range(middle - 1):
            def inwards(p, c, hop=hop):
                return {hop: (p, c + 1), n_pcol - 1 - hop: (p, c - 1)}.get(c)

            came = send(message, inwards)
            message = kernel(functools.partial(join_kernel, size=part_size), out, [VMEM] * 3, VMEM)(part, mine, came)
        across = send(message, lambda p, c: (p, n_pcol - 1 - c) if c in (middle - 1, middle) else None)
        total = kernel(functools.partial(meet_kernel, size=part_size, n_pcol=n_pcol), out, [VMEM] * 2, VMEM)(message, across)
        came, value = None, total
        for hop in range(middle - 1):
            def outwards(p, c, hop=hop):
                return {middle - 1 - hop: (p, c - 1), middle + hop: (p, c + 1)}.get(c)

            value = send(value, outwards)
            came = value if came is None else kernel(add_kernel, out, [VMEM] * 2, VMEM)(came, value)
        return total, came

    part_size = size
    term, sums = None, []
    first = 0
    for k, count in enumerate(chunks):
        message_shape = (count * size + TAIL, width)
        part, message, term = kernel(
            functools.partial(product_kernel, first=first, size=size),
            [pltpu.VMEM((count * size, width), F32), pltpu.VMEM(message_shape, jnp.int16),
             pltpu.VMEM((width, width), F32)],
            [VMEM] * (5 if term is None else 6), [VMEM] * 3,
        )(lefts[k], own, other, a, b, *(() if term is None else (term,)))
        sums.append((first, count, *sum_over_line(part, message)))
        first += count

    half = width // ratio
    shape = pltpu.VMEM((width, half), F32)
    d, give = kernel(functools.partial(halves_kernel, ratio=ratio), [shape] * 2, [VMEM], [VMEM] * 2)(term)
    came = send(give, swap)
    step = ratio
    while True:
        d = kernel(add_kernel, shape, [VMEM] * 2, VMEM)(d, came)
        if step >= n_prow:
            break
        came = send(d, lambda p, c, step=step: (p ^ step, c))
        step *= 2
    part_size = width
    message = kernel(
        lambda x, o: store_message(o, x, width), pltpu.VMEM((width + TAIL, half), jnp.int16), [VMEM], VMEM
    )(d)
    total, came = sum_over_line(d, message)
    mine = kernel(
        functools.partial(pick_kernel, n_pcol=n_pcol), pltpu.VMEM(message.shape, jnp.int16), [VMEM] * 2, VMEM
    )(total, came)
    back = send(mine, swap)
    diagonal_inverse = kernel(
        functools.partial(diagonal_kernel, ratio=ratio), jax.ShapeDtypeStruct((width, width), F32), [VMEM] * 3, VMEM
    )(supernode_inverse, mine, back)

    result = None
    for first, count, total, came in sums:
      result = kernel(
          functools.partial(
              spread_kernel, first=first, size=size, per=per, n_pcol=n_pcol, fill=result is None
          ),
          jax.ShapeDtypeStruct((rows_dev, width), F32),
          [SMEM] * 3 + [VMEM] * 2 + ([] if result is None else [HBM]), HBM,
          scratch_shapes=[
              pltpu.VMEM((count * size, width), F32), pltpu.VMEM((size, width), F32),
              pltpu.SemaphoreType.DMA((count + per,)),
          ],
          input_output_aliases={} if result is None else {5: 0},
      )(rows, valid, block_live, total, came, *(() if result is None else (result,)))
    return result, diagonal_inverse


def solution(mesh):
    n_prow, n_pcol = mesh.shape["prow"], mesh.shape["pcol"]

    def per_device(inverse_trailing, panel, supernode_inverse, block_live):
        per = block_live.shape[0] // n_prow
        smallest = min(per, SMALLEST)

        def program(n):
            def run(*args):
                return packed_step(*args, n=n, n_prow=n_prow, n_pcol=n_pcol)

            return run

        programs = [program(n) for n in range(smallest, per + 1)]
        args = (inverse_trailing, panel, supernode_inverse, block_live)
        if len(programs) == 1:
            return programs[0](*args)
        counts = jnp.sum((block_live != 0).astype(jnp.int32).reshape(n_prow, per), axis=1)
        return lax.switch(jnp.max(counts) - smallest, programs, *args)

    in_specs = (P("prow", "pcol"), P("prow", None), P(), P())
    out_specs = (P("prow", None), P())
    return jax.shard_map(
        per_device, mesh=mesh, in_specs=in_specs, out_specs=out_specs, check_vma=False
    )
```

profile of v0, /device:TPU:0, one launch (start us, length us, event | category | flops | bytes accessed | tf_op | source)
XLA Modules:
  0.0 143.8 jit_solution(15198350578184892454)
XLA Ops:
  0.6 0.6 copy-done.1
  1.3 2.6 %shard_map.59 = (bf16[1280,256]{1,0:T(8,128)(2,1)S(1)}, bf16[1024,256]{1,0:T(8,128)(2,1)S(1)}, bf16[768,256]{1,0:T(8,128)(2,1)S(1)}, bf16[512,256]{1,0:T(8,128)(...) custom-call(s32[72]{0:T(128)S(1)} %copy-done.1, ...), custom_call_target="tpu_custom_call" | custom-call | tf_op jit(solution)/shard_map/pallas_call | solution.py:340
  3.9 4.7 %collective-permute-start.1 = (bf16[512,256]{1,0:T(8,128)(2,1)S(1)}, bf16[512,256]{1,0:T(8,128)(2,1)S(1)}, u32[]{:S(2)}, u32[]{:S(2)}) collective-permute-start(bf16[512,256]{1,0:T(8,128)(2,1)S(1)} %get-tuple-element.31), channel_id=1, source_target_pairs={{0,8},{4,12},{9,1},{13,5},{18,26},{22,30},{27,19},{31,23}} | collective-permute-start | bytes 786440 | tf_op jit(solution)/shard_map/ppermute | solution.py:327
  8.6 1.3 collective-permute-start.9
  9.9 1.3 collective-permute-start
  11.2 1.3 collective-permute-start.4
  12.6 1.3 collective-permute-start.5
  13.9 1.4 collective-permute-done.1.xa2
  15.2 1.3 collective-permute-start.6
  16.5 17.4 %collective-permute-done.xa1 = bf16[768,256]{1,0:T(8,128)(2,1)S(1)} collective-permute-done((bf16[768,256]{1,0:T(8,128)(2,1)S(1)}, bf16[768,256]{1,0:T(8,128)(2,1)S(1)}, u32[]{:S(2)}, u32[]{:S(2)}) %collective-permute-start) | collective-permute-done | bytes 393248 | tf_op jit(solution)/shard_map/ppermute | solution.py:327
  33.9 0.7 collective-permute-start.2
  34.6 0.7 collective-permute-start.3
  35.3 2.6 %collective-permute-done.6.yb2 = bf16[512,256]{1,0:T(8,128)(2,1)S(1)} collective-permute-done((bf16[512,256]{1,0:T(8,128)(2,1)S(1)}, bf16[512,256]{1,0:T(8,128)(2,1)S(1)}, u32[]{:S(2)}, u32[]{:S(2)}) %collective-permute-start.6) | collective-permute-done | bytes 262176 | tf_op jit(solution)/shard_map/ppermute | solution.py:327
  37.9 0.7 collective-permute-start.7
  38.6 0.7 collective-permute-start.8
  39.3 0.1 shard_map.61.own
  39.4 0.1 collective-permute-start.10
  39.5 4.0 %shard_map.64.left = bf16[768,4608]{1,0:T(8,128)(2,1)S(1)} custom-call(s32[9]{0:T(128)S(1)} %get-tuple-element.25.rows, s32[18]{0:T(128)S(1)} %get-tuple-element.27.cols, bf16[2304,4608]{1,0:T(8,128)(2,1)} %a.7), custom_call_target="tpu_custom_call" | custom-call | tf_op jit(solution)/shard_map/pallas_call | solution.py:361
  43.5 4.3 %shard_map.63.left = bf16[768,4608]{1,0:T(8,128)(2,1)S(1)} custom-call(s32[9]{0:T(128)S(1)} %get-tuple-element.25.rows, s32[18]{0:T(128)S(1)} %get-tuple-element.27.cols, bf16[2304,4608]{1,0:T(8,128)(2,1)} %a.7), custom_call_target="tpu_custom_call" | custom-call | tf_op jit(solution)/shard_map/pallas_call | solution.py:361
  47.9 3.0 %shard_map.65 = (f32[768,256]{1,0:T(8,128)S(1)}, s16[784,256]{1,0:T(8,128)(2,1)S(1)}, f32[256,256]{1,0:T(8,128)S(1)}) custom-call(bf16[768,4608]{1,0:T(8,128)(2,1)S(1)} %shard_map.64.left, bf16[2304,256]{1,0:T(8,128)(2,1)S(1)} %shard_map.61.own, bf16[2304,256]{1,0:T(8,128)(2,1)S(1)} %collective-permute-done.10.other, ...), custom_call_target="tpu_custom_call" | custom-call | tf_op jit(solution)/shard_map/pallas_call | solution.py:423
  50.9 14.5 %collective-permute-start.20 = (s16[784,256]{1,0:T(8,128)(2,1)S(1)}, s16[784,256]{1,0:T(8,128)(2,1)S(1)}, u32[]{:S(2)}, u32[]{:S(2)}) collective-permute-start(s16[784,256]{1,0:T(8,128)(2,1)S(1)} %get-tuple-element.44.mine), channel_id=1, source_target_pairs={{0,1},{3,2},{4,5},{7,6},{8,9},{11,10},{12,13},{15,14},{16,17},{19,... | collective-permute-start | bytes 1204232 | tf_op jit(solution)/shard_map/ppermute | solution.py:327
  65.4 3.0 %shard_map.66 = (f32[768,256]{1,0:T(8,128)S(1)}, s16[784,256]{1,0:T(8,128)(2,1)S(1)}, f32[256,256]{1,0:T(8,128)S(1)}) custom-call(bf16[768,4608]{1,0:T(8,128)(2,1)S(1)} %shard_map.63.left, bf16[2304,256]{1,0:T(8,128)(2,1)S(1)} %shard_map.61.own, bf16[2304,256]{1,0:T(8,128)(2,1)S(1)} %collective-permute-done.10.other, ...), custom_call_target="tpu_custom_call" | custom-call | tf_op jit(solution)/shard_map/pallas_call | solution.py:423
  68.4 1.3 collective-permute-start.17
  69.7 4.0 %shard_map.62.left = bf16[512,4608]{1,0:T(8,128)(2,1)S(1)} custom-call(s32[9]{0:T(128)S(1)} %get-tuple-element.25.rows, s32[18]{0:T(128)S(1)} %get-tuple-element.27.cols, bf16[2304,4608]{1,0:T(8,128)(2,1)} %a.7), custom_call_target="tpu_custom_call" | custom-call | tf_op jit(solution)/shard_map/pallas_call | solution.py:361
  73.8 2.1 %shard_map.67 = (f32[512,256]{1,0:T(8,128)S(1)}, s16[528,256]{1,0:T(8,128)(2,1)S(1)}, f32[256,256]{1,0:T(8,128)S(1)}) custom-call(bf16[512,4608]{1,0:T(8,128)(2,1)S(1)} %shard_map.62.left, bf16[2304,256]{1,0:T(8,128)(2,1)S(1)} %shard_map.61.own, bf16[2304,256]{1,0:T(8,128)(2,1)S(1)} %collective-permute-done.10.other, ...), custom_call_target="tpu_custom_call" | custom-call | tf_op jit(solution)/shard_map/pallas_call | solution.py:423
  75.9 1.8 %collective-permute-start.14 = (s16[528,256]{1,0:T(8,128)(2,1)S(1)}, s16[528,256]{1,0:T(8,128)(2,1)S(1)}, u32[]{:S(2)}, u32[]{:S(2)}) collective-permute-start(s16[528,256]{1,0:T(8,128)(2,1)S(1)} %get-tuple-element.40.mine), channel_id=1, source_target_pairs={{0,1},{3,2},{4,5},{7,6},{8,9},{11,10},{12,13},{15,14},{16,17},{19,... | collective-permute-start | bytes 811016 | tf_op jit(solution)/shard_map/ppermute | solution.py:327
  77.7 0.3 shard_map.75.mine
  78.0 0.7 collective-permute-start.21
  78.6 5.0 %collective-permute-done.17.came = s16[784,256]{1,0:T(8,128)(2,1)S(1)} collective-permute-done((s16[784,256]{1,0:T(8,128)(2,1)S(1)}, s16[784,256]{1,0:T(8,128)(2,1)S(1)}, u32[]{:S(2)}, u32[]{:S(2)}) %collective-permute-start.17) | collective-permute-done | bytes 401440 | tf_op jit(solution)/shard_map/ppermute | solution.py:327
  83.6 0.3 shard_map.73.mine
  83.9 0.7 collective-permute-start.18
  84.6 2.6 %shard_map.60.left = bf16[256,4608]{1,0:T(8,128)(2,1)S(1)} custom-call(s32[9]{0:T(128)S(1)} %get-tuple-element.25.rows, s32[18]{0:T(128)S(1)} %get-tuple-element.27.cols, bf16[2304,4608]{1,0:T(8,128)(2,1)} %a.7), custom_call_target="tpu_custom_call" | custom-call | tf_op jit(solution)/shard_map/pallas_call | solution.py:361
  87.2 1.2 shard_map.68
  88.6 1.3 collective-permute-done.23.y
  89.9 0.1 collective-permute-start.24
  90.0 0.2 shard_map.71.mine
  90.2 0.7 collective-permute-start.15
  90.9 15.2 %collective-permute-start.11 = (s16[272,256]{1,0:T(8,128)(2,1)S(1)}, s16[272,256]{1,0:T(8,128)(2,1)S(1)}, u32[]{:S(2)}, u32[]{:S(2)}) collective-permute-start(s16[272,256]{1,0:T(8,128)(2,1)S(1)} %get-tuple-element.38.mine), channel_id=1, source_target_pairs={{0,1},{3,2},{4,5},{7,6},{8,9},{11,10},{12,13},{15,14},{16,17},{19,... | collective-permute-start | bytes 417800 | tf_op jit(solution)/shard_map/ppermute | solution.py:327
  106.1 0.1 collective-permute-start.25
  106.2 0.4 shard_map.76.total
  106.6 1.4 collective-permute-start.22
  108.1 0.4 shard_map.74.total
  108.5 1.3 collective-permute-start.19
  109.8 1.4 collective-permute-done.25.y
  111.1 0.1 shard_map.85.mine
  111.2 3.3 %collective-permute-start.26 = (s16[272,128]{1,0:T(8,128)(2,1)S(1)}, s16[272,128]{1,0:T(8,128)(2,1)S(1)}, u32[]{:S(2)}, u32[]{:S(2)}) collective-permute-start(s16[272,128]{1,0:T(8,128)(2,1)S(1)} %shard_map.85.mine), channel_id=1, source_target_pairs={{0,1},{3,2},{4,5},{7,6},{8,9},{11,10},{12,13},{15,14},{16,17},{19,... | collective-permute-start | bytes 208904 | tf_op jit(solution)/shard_map/ppermute | solution.py:327
  114.5 0.1 shard_map.69.mine
  114.6 0.7 collective-permute-start.12
  115.3 0.3 shard_map.72.total
  115.6 1.3 collective-permute-start.16
  116.9 0.1 shard_map.86.mine
  117.0 0.7 collective-permute-start.27
  117.7 0.1 shard_map.87.total
  117.8 1.3 collective-permute-start.28
  119.1 0.2 shard_map.70.total
  119.3 1.3 collective-permute-start.13
  120.6 16.1 %collective-permute-done.28.came = s16[272,128]{1,0:T(8,128)(2,1)S(1)} collective-permute-done((s16[272,128]{1,0:T(8,128)(2,1)S(1)}, s16[272,128]{1,0:T(8,128)(2,1)S(1)}, u32[]{:S(2)}, u32[]{:S(2)}) %collective-permute-start.28) | collective-permute-done | bytes 69664 | tf_op jit(solution)/shard_map/ppermute | solution.py:327
  136.7 0.1 collective-permute-start.29
  136.8 1.2 collective-permute-done.29.other
  138.1 0.8 shard_map.89
  138.8 1.8 %shard_map.77.refs_0_ = f32[2304,256]{1,0:T(8,128)} custom-call(s32[9]{0:T(128)S(1)} %get-tuple-element.25.rows, s32[9]{0:T(128)S(1)} %get-tuple-element.26.valid, s32[72]{0:T(128)S(1)} %copy-done.2, s16[784,256]{1,0:T(8,128)(2,1)S(1)} %shard_map.76.total, s16[784,256]{1,0:T(8,128)(2,1)S(1)} %collective-permute-done.22.came), custom_call_target="tpu_custom_call" | custom-call | tf_op jit(solution)/shard_map/pallas_call | solution.py:458
  140.7 1.6 %shard_map.78.refs_0_ = f32[2304,256]{1,0:T(8,128)} custom-call(s32[9]{0:T(128)S(1)} %get-tuple-element.25.rows, s32[9]{0:T(128)S(1)} %get-tuple-element.26.valid, s32[72]{0:T(128)S(1)} %copy-done.2, s16[784,256]{1,0:T(8,128)(2,1)S(1)} %shard_map.74.total, s16[784,256]{1,0:T(8,128)(2,1)S(1)} %collective-permute-done.19.came, ...), custom_call_target="tpu_custom_call", output_to_operand_aliasing={{}: (5, {})} | custom-call | tf_op jit(solution)/shard_map/pallas_call | solution.py:458
  142.3 0.8 shard_map.79.refs_0_
  143.1 0.7 shard_map.80
  (33 shorter events, 0.3 us)
Async XLA Ops:
  0.6 0.7 copy-start.1
  3.9 11.3 %collective-permute-start.1 = (bf16[512,256]{1,0:T(8,128)(2,1)S(1)}, bf16[512,256]{1,0:T(8,128)(2,1)S(1)}, u32[]{:S(2)}, u32[]{:S(2)}) collective-permute-start(bf16[512,256]{1,0:T(8,128)(2,1)S(1)} %get-tuple-element.31), channel_id=1, source_target_pairs={{0,8},{4,12},{9,1},{13,5},{18,26},{22,30},{27,19},{31,23}} | collective-permute-start | bytes 786440 | tf_op jit(solution)/shard_map/ppermute | solution.py:327
  8.6 30.0 %collective-permute-start.9 = (bf16[1024,256]{1,0:T(8,128)(2,1)S(1)}, bf16[1024,256]{1,0:T(8,128)(2,1)S(1)}, u32[]{:S(2)}, u32[]{:S(2)}) collective-permute-start(bf16[1024,256]{1,0:T(8,128)(2,1)S(1)} %get-tuple-element.29.b), channel_id=1, source_target_pairs={{0,8},{4,12},{9,1},{13,5},{18,26},{22,30},{27,19},{31,23}} | collective-permute-start | bytes 1572872 | tf_op jit(solution)/shard_map/ppermute | solution.py:327
  9.9 24.0 %collective-permute-start = (bf16[768,256]{1,0:T(8,128)(2,1)S(1)}, bf16[768,256]{1,0:T(8,128)(2,1)S(1)}, u32[]{:S(2)}, u32[]{:S(2)}) collective-permute-start(bf16[768,256]{1,0:T(8,128)(2,1)S(1)} %get-tuple-element.30), channel_id=1, source_target_pairs={{0,8},{4,12},{9,1},{13,5},{18,26},{22,30},{27,19},{31,23}} | collective-permute-start | bytes 1179656 | tf_op jit(solution)/shard_map/ppermute | solution.py:327
  11.2 28.1 %collective-permute-start.4 = (bf16[1280,256]{1,0:T(8,128)(2,1)S(1)}, bf16[1280,256]{1,0:T(8,128)(2,1)S(1)}, u32[]{:S(2)}, u32[]{:S(2)}) collective-permute-start(bf16[1280,256]{1,0:T(8,128)(2,1)S(1)} %get-tuple-element.28.a), channel_id=1, source_target_pairs={{0,16},{4,20},{9,25},{13,29},{18,2},{22,6},{27,11},{31,15}} | collective-permute-start | bytes 1966088 | tf_op jit(solution)/shard_map/ppermute | solution.py:327
  12.6 22.0 %collective-permute-start.5 = (bf16[512,256]{1,0:T(8,128)(2,1)S(1)}, bf16[512,256]{1,0:T(8,128)(2,1)S(1)}, u32[]{:S(2)}, u32[]{:S(2)}) collective-permute-start(bf16[512,256]{1,0:T(8,128)(2,1)S(1)} %get-tuple-element.32), channel_id=1, source_target_pairs={{0,16},{4,20},{9,25},{13,29},{18,2},{22,6},{27,11},{31,15}} | collective-permute-start | bytes 786440 | tf_op jit(solution)/shard_map/ppermute | solution.py:327
  15.2 22.6 %collective-permute-start.6 = (bf16[512,256]{1,0:T(8,128)(2,1)S(1)}, bf16[512,256]{1,0:T(8,128)(2,1)S(1)}, u32[]{:S(2)}, u32[]{:S(2)}) collective-permute-start(bf16[512,256]{1,0:T(8,128)(2,1)S(1)} %get-tuple-element.33), channel_id=1, source_target_pairs={{0,16},{4,20},{9,25},{13,29},{18,2},{22,6},{27,11},{31,15}} | collective-permute-start | bytes 786440 | tf_op jit(solution)/shard_map/ppermute | solution.py:327
  33.9 5.4 %collective-permute-start.2 = (bf16[768,256]{1,0:T(8,128)(2,1)S(1)}, bf16[768,256]{1,0:T(8,128)(2,1)S(1)}, u32[]{:S(2)}, u32[]{:S(2)}) collective-permute-start(bf16[768,256]{1,0:T(8,128)(2,1)S(1)} %collective-permute-done.xa1), channel_id=1, source_target_pairs={{1,17},{5,21},{8,24},{12,28},{19,3},{23,7},{26,10},{30,14}} | collective-permute-start | bytes 1179656 | tf_op jit(solution)/shard_map/ppermute | solution.py:327
  34.6 4.6 %collective-permute-start.3 = (bf16[512,256]{1,0:T(8,128)(2,1)S(1)}, bf16[512,256]{1,0:T(8,128)(2,1)S(1)}, u32[]{:S(2)}, u32[]{:S(2)}) collective-permute-start(bf16[512,256]{1,0:T(8,128)(2,1)S(1)} %collective-permute-done.1.xa2), channel_id=1, source_target_pairs={{1,17},{5,21},{8,24},{12,28},{19,3},{23,7},{26,10},{30,14}} | collective-permute-start | bytes 786440 | tf_op jit(solution)/shard_map/ppermute | solution.py:327
  37.9 1.4 collective-permute-start.7
  38.6 0.7 collective-permute-start.8
  39.4 8.4 %collective-permute-start.10 = (bf16[2304,256]{1,0:T(8,128)(2,1)S(1)}, bf16[2304,256]{1,0:T(8,128)(2,1)S(1)}, u32[]{:S(2)}, u32[]{:S(2)}) collective-permute-start(bf16[2304,256]{1,0:T(8,128)(2,1)S(1)} %shard_map.61.own), channel_id=1, source_target_pairs={{0,4},{1,5},{2,6},{3,7},{4,0},{5,1},{6,2},{7,3},{8,12},{9,13},{10,... | collective-permute-start | bytes 3538952 | tf_op jit(solution)/shard_map/ppermute | solution.py:327
  50.9 26.8 %collective-permute-start.20 = (s16[784,256]{1,0:T(8,128)(2,1)S(1)}, s16[784,256]{1,0:T(8,128)(2,1)S(1)}, u32[]{:S(2)}, u32[]{:S(2)}) collective-permute-start(s16[784,256]{1,0:T(8,128)(2,1)S(1)} %get-tuple-element.44.mine), channel_id=1, source_target_pairs={{0,1},{3,2},{4,5},{7,6},{8,9},{11,10},{12,13},{15,14},{16,17},{19,... | collective-permute-start | bytes 1204232 | tf_op jit(solution)/shard_map/ppermute | solution.py:327
  68.4 15.2 %collective-permute-start.17 = (s16[784,256]{1,0:T(8,128)(2,1)S(1)}, s16[784,256]{1,0:T(8,128)(2,1)S(1)}, u32[]{:S(2)}, u32[]{:S(2)}) collective-permute-start(s16[784,256]{1,0:T(8,128)(2,1)S(1)} %get-tuple-element.42.mine), channel_id=1, source_target_pairs={{0,1},{3,2},{4,5},{7,6},{8,9},{11,10},{12,13},{15,14},{16,17},{19,... | collective-permute-start | bytes 1204232 | tf_op jit(solution)/shard_map/ppermute | solution.py:327
  75.9 14.1 %collective-permute-start.14 = (s16[528,256]{1,0:T(8,128)(2,1)S(1)}, s16[528,256]{1,0:T(8,128)(2,1)S(1)}, u32[]{:S(2)}, u32[]{:S(2)}) collective-permute-start(s16[528,256]{1,0:T(8,128)(2,1)S(1)} %get-tuple-element.40.mine), channel_id=1, source_target_pairs={{0,1},{3,2},{4,5},{7,6},{8,9},{11,10},{12,13},{15,14},{16,17},{19,... | collective-permute-start | bytes 811016 | tf_op jit(solution)/shard_map/ppermute | solution.py:327
  78.0 28.2 %collective-permute-start.21 = (s16[784,256]{1,0:T(8,128)(2,1)S(1)}, s16[784,256]{1,0:T(8,128)(2,1)S(1)}, u32[]{:S(2)}, u32[]{:S(2)}) collective-permute-start(s16[784,256]{1,0:T(8,128)(2,1)S(1)} %shard_map.75.mine), channel_id=1, source_target_pairs={{1,2},{2,1},{5,6},{6,5},{9,10},{10,9},{13,14},{14,13},{17,18},{18,... | collective-permute-start | bytes 1204232 | tf_op jit(solution)/shard_map/ppermute | solution.py:327
  83.9 24.2 %collective-permute-start.18 = (s16[784,256]{1,0:T(8,128)(2,1)S(1)}, s16[784,256]{1,0:T(8,128)(2,1)S(1)}, u32[]{:S(2)}, u32[]{:S(2)}) collective-permute-start(s16[784,256]{1,0:T(8,128)(2,1)S(1)} %shard_map.73.mine), channel_id=1, source_target_pairs={{1,2},{2,1},{5,6},{6,5},{9,10},{10,9},{13,14},{14,13},{17,18},{18,... | collective-permute-start | bytes 1204232 | tf_op jit(solution)/shard_map/ppermute | solution.py:327
  88.5 1.4 collective-permute-start.23
  89.9 16.1 %collective-permute-start.24 = (f32[256,128]{1,0:T(8,128)S(1)}, f32[256,128]{1,0:T(8,128)S(1)}, u32[]{:S(2)}, u32[]{:S(2)}) collective-permute-start(f32[256,128]{1,0:T(8,128)S(1)} %shard_map.82.x), channel_id=1, source_target_pairs={{0,8},{1,9},{2,10},{3,11},{4,12},{5,13},{6,14},{7,15},{8,0},{9,1},... | collective-permute-start | bytes 393224 | tf_op jit(solution)/shard_map/ppermute | solution.py:327
  90.2 25.1 %collective-permute-start.15 = (s16[528,256]{1,0:T(8,128)(2,1)S(1)}, s16[528,256]{1,0:T(8,128)(2,1)S(1)}, u32[]{:S(2)}, u32[]{:S(2)}) collective-permute-start(s16[528,256]{1,0:T(8,128)(2,1)S(1)} %shard_map.71.mine), channel_id=1, source_target_pairs={{1,2},{2,1},{5,6},{6,5},{9,10},{10,9},{13,14},{14,13},{17,18},{18,... | collective-permute-start | bytes 811016 | tf_op jit(solution)/shard_map/ppermute | solution.py:327
  90.9 23.6 %collective-permute-start.11 = (s16[272,256]{1,0:T(8,128)(2,1)S(1)}, s16[272,256]{1,0:T(8,128)(2,1)S(1)}, u32[]{:S(2)}, u32[]{:S(2)}) collective-permute-start(s16[272,256]{1,0:T(8,128)(2,1)S(1)} %get-tuple-element.38.mine), channel_id=1, source_target_pairs={{0,1},{3,2},{4,5},{7,6},{8,9},{11,10},{12,13},{15,14},{16,17},{19,... | collective-permute-start | bytes 417800 | tf_op jit(solution)/shard_map/ppermute | solution.py:327
  106.1 5.0 %collective-permute-start.25 = (f32[256,128]{1,0:T(8,128)S(1)}, f32[256,128]{1,0:T(8,128)S(1)}, u32[]{:S(2)}, u32[]{:S(2)}) collective-permute-start(f32[256,128]{1,0:T(8,128)S(1)} %shard_map.83.x), channel_id=1, source_target_pairs={{0,16},{1,17},{2,18},{3,19},{4,20},{5,21},{6,22},{7,23},{8,24},{9,... | collective-permute-start | bytes 393224 | tf_op jit(solution)/shard_map/ppermute | solution.py:327
  106.6 31.5 %copy-start = (f32[256,256]{1,0:T(8,128)S(1)}, f32[256,256]{1,0:T(8,128)}, u32[]{:S(2)}) copy-start(f32[256,256]{1,0:T(8,128)} %base.1) | copy-start | bytes 786436
  106.6 32.2 %copy-start.2 = (s32[72]{0:T(128)S(1)}, s32[72]{0:T(128)}, u32[]{:S(2)}) copy-start(s32[72]{0:T(128)} %live.9) | copy-start | bytes 868
  106.6 32.2 %collective-permute-start.22 = (s16[784,256]{1,0:T(8,128)(2,1)S(1)}, s16[784,256]{1,0:T(8,128)(2,1)S(1)}, u32[]{:S(2)}, u32[]{:S(2)}) collective-permute-start(s16[784,256]{1,0:T(8,128)(2,1)S(1)} %shard_map.76.total), channel_id=1, source_target_pairs={{1,0},{2,3},{5,4},{6,7},{9,8},{10,11},{13,12},{14,15},{17,16},{18,... | collective-permute-start | bytes 1204232 | tf_op jit(solution)/shard_map/ppermute | solution.py:327
  108.5 32.2 %collective-permute-start.19 = (s16[784,256]{1,0:T(8,128)(2,1)S(1)}, s16[784,256]{1,0:T(8,128)(2,1)S(1)}, u32[]{:S(2)}, u32[]{:S(2)}) collective-permute-start(s16[784,256]{1,0:T(8,128)(2,1)S(1)} %shard_map.74.total), channel_id=1, source_target_pairs={{1,0},{2,3},{5,4},{6,7},{9,8},{10,11},{13,12},{14,15},{17,16},{18,... | collective-permute-start | bytes 1204232 | tf_op jit(solution)/shard_map/ppermute | solution.py:327
  111.2 5.7 %collective-permute-start.26 = (s16[272,128]{1,0:T(8,128)(2,1)S(1)}, s16[272,128]{1,0:T(8,128)(2,1)S(1)}, u32[]{:S(2)}, u32[]{:S(2)}) collective-permute-start(s16[272,128]{1,0:T(8,128)(2,1)S(1)} %shard_map.85.mine), channel_id=1, source_target_pairs={{0,1},{3,2},{4,5},{7,6},{8,9},{11,10},{12,13},{15,14},{16,17},{19,... | collective-permute-start | bytes 208904 | tf_op jit(solution)/shard_map/ppermute | solution.py:327
  114.6 4.5 %collective-permute-start.12 = (s16[272,256]{1,0:T(8,128)(2,1)S(1)}, s16[272,256]{1,0:T(8,128)(2,1)S(1)}, u32[]{:S(2)}, u32[]{:S(2)}) collective-permute-start(s16[272,256]{1,0:T(8,128)(2,1)S(1)} %shard_map.69.mine), channel_id=1, source_target_pairs={{1,2},{2,1},{5,6},{6,5},{9,10},{10,9},{13,14},{14,13},{17,18},{18,... | collective-permute-start | bytes 417800 | tf_op jit(solution)/shard_map/ppermute | solution.py:327
  115.6 26.7 %collective-permute-start.16 = (s16[528,256]{1,0:T(8,128)(2,1)S(1)}, s16[528,256]{1,0:T(8,128)(2,1)S(1)}, u32[]{:S(2)}, u32[]{:S(2)}) collective-permute-start(s16[528,256]{1,0:T(8,128)(2,1)S(1)} %shard_map.72.total), channel_id=1, source_target_pairs={{1,0},{2,3},{5,4},{6,7},{9,8},{10,11},{13,12},{14,15},{17,16},{18,... | collective-permute-start | bytes 811016 | tf_op jit(solution)/shard_map/ppermute | solution.py:327
  117.0 0.7 collective-permute-start.27
  117.8 18.9 %collective-permute-start.28 = (s16[272,128]{1,0:T(8,128)(2,1)S(1)}, s16[272,128]{1,0:T(8,128)(2,1)S(1)}, u32[]{:S(2)}, u32[]{:S(2)}) collective-permute-start(s16[272,128]{1,0:T(8,128)(2,1)S(1)} %shard_map.87.total), channel_id=1, source_target_pairs={{1,0},{2,3},{5,4},{6,7},{9,8},{10,11},{13,12},{14,15},{17,16},{18,... | collective-permute-start | bytes 208904 | tf_op jit(solution)/shard_map/ppermute | solution.py:327
  119.3 23.8 %collective-permute-start.13 = (s16[272,256]{1,0:T(8,128)(2,1)S(1)}, s16[272,256]{1,0:T(8,128)(2,1)S(1)}, u32[]{:S(2)}, u32[]{:S(2)}) collective-permute-start(s16[272,256]{1,0:T(8,128)(2,1)S(1)} %shard_map.70.total), channel_id=1, source_target_pairs={{1,0},{2,3},{5,4},{6,7},{9,8},{10,11},{13,12},{14,15},{17,16},{18,... | collective-permute-start | bytes 417800 | tf_op jit(solution)/shard_map/ppermute | solution.py:327
  136.7 1.3 collective-permute-start.29
where the time goes:
time: 144 us
  starting transfers between devices  60.2 us (42%)
  waiting for transfers between devices  46.4 us (32%)
  Pallas kernels  35.3 us (25%)
    ppermute x30, starting transfers between devices, send(): return near(lax.ppermute(value, AXES, pairs))  60.2 us
    ppermute x30, waiting for transfers between devices, send(): return near(lax.ppermute(value, AXES, pairs))  46.4 us
    pallas_call x4, Pallas kernels, packed_step(): kernel(functools.partial(fetch_kernel, first=first, size=size), pltpu.VME...  15 us
    pallas_call x4, Pallas kernels, packed_step(): kernel(functools.partial(product_kernel, first=first, size=size), [pltpu....  9.36 us
    pallas_call x4, Pallas kernels, packed_step(): kernel(functools.partial(spread_kernel, first=first, size=size, per=per,...  4.96 us
  transfers between devices with their start and end apart: 30, of which 8 were waited for; matrix products, arithmetic and copies ran while one was open for 0% of the time, Pallas kernels for 20%

commit v1 on v0

--- a/solution.py
+++ b/solution.py
@@ -9,7 +9,7 @@
 
 
 AXES = ("prow", "pcol")
-SMALLEST = 9
+SMALLEST = 7
 SCRATCH = 8 << 20
 ROWS = 64
 TAIL = 16
@@ -65,6 +65,10 @@
     lax.fori_loop(0, size // ROWS, one, 0)
 
 
+def rows_from(start, r):
+    return pl.ds(pl.multiple_of(start + r * ROWS, ROWS), ROWS)
+
+
 def rows_at(block, r, size):
     return pl.ds(pl.multiple_of(block * size + r * ROWS, ROWS), ROWS)
 
@@ -172,8 +176,12 @@
 
     @pl.when(root)
     def _():
-        full[: a.shape[0], :] = a[...]
-        full[a.shape[0] :, :] = b[...]
+        for source, to in ((a, 0), (b, a.shape[0])):
+
+            def one(r, source=source, to=to):
+                full[rows_from(to, r), :] = source[rows_from(0, r), :]
+
+            by_rows(source.shape[0], one)
 
     @pl.when(jnp.logical_not(root))
     def _():
@@ -181,17 +189,27 @@
         for whole, early, late in ((ya, (xa1, xa2), (da1, da2)), (xb, (yb1, yb2), (db1, db2))):
             inner = 0
             for e, l in zip(early, late):
-                size = e.shape[0]
-                full[start : start + size, :] = whole[inner : inner + size, :] + e[...] + l[...]
-                start += size
-                inner += size
+
+                def one(r, whole=whole, e=e, l=l, start=start, inner=inner):
+                    at = rows_from(0, r)
+                    full[rows_from(start, r), :] = whole[rows_from(inner, r), :] + e[at, :] + l[at, :]
+
+                by_rows(e.shape[0], one)
+                start += e.shape[0]
+                inner += e.shape[0]
 
 
 def product_kernel(left, own, other, a, b, *refs, first, size):
     part, message, term = refs[-3:]
     n_rows = own.shape[0]
-    acc = jnp.dot(left[:, :n_rows], own[...], preferred_element_type=F32)
-    part[...] = acc + jnp.dot(left[:, n_rows:], other[...], preferred_element_type=F32)
+
+    def one(i, _):
+        at = pl.ds(pl.multiple_of(i * size, size), size)
+        acc = jnp.dot(left[at, :n_rows], own[...], preferred_element_type=F32)
+        part[at, :] = acc + jnp.dot(left[at, n_rows:], other[...], preferred_element_type=F32)
+        return 0
+
+    lax.fori_loop(0, left.shape[0] // size, one, 0)
     store_message(message, part, size)
     contract = (((0,), (0,)), ((), ()))
     total = refs[0][...] if len(refs) == 4 else None
@@ -276,6 +294,16 @@
     out[...] = jnp.where(is_middle(n_pcol), total[...], came[...])
 
 
+def capacity_kernel(live, out, *, groups, per):
+    most = 0
+    for g in range(groups):
+        count = 0
+        for k in range(per):
+            count = count + (live[g * per + k] != 0).astype(jnp.int32)
+        most = jnp.maximum(most, count)
+    out[0] = most
+
+
 def add_kernel(x, y, out):
     out[...] = x[...] + y[...]
 
@@ -307,7 +335,7 @@
 
 
 def chunk_sizes(n):
-    return {9: (3, 3, 2, 1), 8: (3, 2, 2, 1), 7: (3, 2, 1, 1), 6: (2, 2, 1, 1), 5: (2, 2, 1)}.get(n, (n,))
+    return {9: (3, 2, 2, 2), 8: (2, 2, 2, 2), 7: (2, 2, 2, 1)}.get(n, (n,))
 
 
 def packed_step(inverse_trailing, panel, supernode_inverse, block_live, *, n, n_prow, n_pcol):
@@ -487,8 +515,11 @@
         args = (inverse_trailing, panel, supernode_inverse, block_live)
         if len(programs) == 1:
             return programs[0](*args)
-        counts = jnp.sum((block_live != 0).astype(jnp.int32).reshape(n_prow, per), axis=1)
-        return lax.switch(jnp.max(counts) - smallest, programs, *args)
+        most = kernel(
+            functools.partial(capacity_kernel, groups=n_prow, per=per),
+            jax.ShapeDtypeStruct((1,), jnp.int32), [SMEM], SMEM,
+        )(block_live)
+        return lax.switch(most[0] - smallest, programs, *args)
 
     in_specs = (P("prow", "pcol"), P("prow", None), P(), P())
     out_specs = (P("prow", None), P())

time: 144 us -> 121 us (0.84)
  starting transfers between devices: 60.2 us -> 46.9 us
  Pallas kernels: 35.3 us -> 27.4 us
  waiting for transfers between devices: 46.4 us -> 43.2 us
    ppermute x30, starting transfers between devices: 60.2 us -> 46.9 us  [send(): return near(lax.ppermute(value, AXES, pairs))]
    pallas_call x4, Pallas kernels: 15 us -> 10.3 us  [packed_step(): kernel(functools.partial(fetch_kernel, first=first, size=size), pltpu.VME...]
    ppermute x30, waiting for transfers between devices: 46.4 us -> 43.2 us  [send(): return near(lax.ppermute(value, AXES, pairs))]
    pallas_call x4, Pallas kernels: 9.36 us -> 6.52 us  [packed_step(): kernel(functools.partial(product_kernel, first=first, size=size), [pltpu....]
    pallas_call x4, Pallas kernels: 4.96 us -> 3.45 us  [packed_step(): kernel(functools.partial(spread_kernel, first=first, size=size, per=per,...]
  transfers between devices with their start and end apart: 30 -> 30, of which waited for: 8 -> 9; matrix products, arithmetic and copies ran while one was open for 0% -> 0% of each run, Pallas kernels for 20% -> 17%
where the time goes in v1:
time: 121 us
  starting transfers between devices  46.9 us (39%)
  waiting for transfers between devices  43.2 us (36%)
  Pallas kernels  27.4 us (23%)
  local copies, waits for them, and re-layouts  1.41 us (1%)
  between operations  1.29 us (1%)
    ppermute x30, starting transfers between devices, send(): return near(lax.ppermute(value, AXES, pairs))  46.9 us
    ppermute x30, waiting for transfers between devices, send(): return near(lax.ppermute(value, AXES, pairs))  43.2 us
    pallas_call x4, Pallas kernels, packed_step(): kernel(functools.partial(fetch_kernel, first=first, size=size), pltpu.VME...  10.3 us
    pallas_call x4, Pallas kernels, packed_step(): kernel(functools.partial(product_kernel, first=first, size=size), [pltpu....  6.52 us
    pallas_call x4, Pallas kernels, packed_step(): kernel(functools.partial(spread_kernel, first=first, size=size, per=per,...  3.45 us
    pallas_call x1, Pallas kernels, packed_step(): kernel(functools.partial(pack_kernel, ranges=ranges, n=n, per=per, ratio=...  2.75 us
  transfers between devices with their start and end apart: 30, of which 9 were waited for; matrix products, arithmetic and copies ran while one was open for 0% of the time, Pallas kernels for 17%

profile of v1, /device:TPU:0, one launch (start us, length us, event | category | flops | bytes accessed | tf_op | source)
XLA Modules:
  0.0 120.8 jit_solution(10924536362408932576)
XLA Ops:
  0.6 1.3 %shard_map.74 = s32[1]{0:T(128)} custom-call(s32[72]{0:T(128)} %live.1), custom_call_target="tpu_custom_call" | custom-call | tf_op jit(solution)/shard_map/pallas_call | solution.py:518
  2.6 118.2 %conditional.1 = (f32[2304,256]{1,0:T(8,128)}, f32[256,256]{1,0:T(8,128)}) conditional(s32[]{:T(128)} %bitcast, (s32[72]{0:T(128)}, bf16[2304,256]{1,0:T(8,128)(2,1)}, bf16[2304,4608]{1,0:T(8,128)(2,1)}, f32[256,256]{1,0:T(8,128)}) %tuple.19, (s32[72]{0:T(128)}, bf16[2304,256]{1,0:T(8,128)(2,1)}, bf16[2304,4608]{1,0:T(8,128)(2,1)}, ...), branch_computations={%region_0.0_spmd, %region_1.0_spmd, %region_2.0_spmd} | conditional | bytes 46598548 | solution.py:522
  2.6 2.8 %branch_0_fun.31 = (bf16[1024,256]{1,0:T(8,128)(2,1)S(1)}, bf16[768,256]{1,0:T(8,128)(2,1)S(1)}, bf16[512,256]{1,0:T(8,128)(2,1)S(1)}, bf16[512,256]{1,0:T(8,128...) custom-call(s32[72]{0:T(128)} %get-tuple-element.24.live, ...), custom_call_target="tpu_custom_call" | custom-call | tf_op jit(solution)/shard_map/cond/branch_0_fun/pallas_call | solution.py:368
  5.3 4.7 %collective-permute-start = (bf16[512,256]{1,0:T(8,128)(2,1)S(1)}, bf16[512,256]{1,0:T(8,128)(2,1)S(1)}, u32[]{:S(2)}, u32[]{:S(2)}) collective-permute-start(bf16[512,256]{1,0:T(8,128)(2,1)S(1)} %get-tuple-element.32), channel_id=1, source_target_pairs={{0,8},{4,12},{9,1},{13,5},{18,26},{22,30},{27,19},{31,23}} | collective-permute-start | bytes 786440 | tf_op jit(solution)/shard_map/cond/branch_0_fun/ppermute | solution.py:355
  10.0 1.3 %collective-permute-start.4 = (bf16[1024,256]{1,0:T(8,128)(2,1)S(1)}, bf16[1024,256]{1,0:T(8,128)(2,1)S(1)}, u32[]{:S(2)}, u32[]{:S(2)}) collective-permute-start(bf16[1024,256]{1,0:T(8,128)(2,1)S(1)} %get-tuple-element.30.a), channel_id=1, source_target_pairs={{0,16},{4,20},{9,25},{13,29},{18,2},{22,6},{27,11},{31,15}} | collective-permute-start | bytes 1572872 | tf_op jit(solution)/shard_map/cond/branch_0_fun/ppermute | solution.py:355
  11.3 1.3 %collective-permute-start.6 = (bf16[256,256]{1,0:T(8,128)(2,1)S(1)}, bf16[256,256]{1,0:T(8,128)(2,1)S(1)}, u32[]{:S(2)}, u32[]{:S(2)}) collective-permute-start(bf16[256,256]{1,0:T(8,128)(2,1)S(1)} %get-tuple-element.35), channel_id=1, source_target_pairs={{0,16},{4,20},{9,25},{13,29},{18,2},{22,6},{27,11},{31,15}} | collective-permute-start | bytes 393224 | tf_op jit(solution)/shard_map/cond/branch_0_fun/ppermute | solution.py:355
  12.6 1.3 %collective-permute-start.1 = (bf16[512,256]{1,0:T(8,128)(2,1)S(1)}, bf16[512,256]{1,0:T(8,128)(2,1)S(1)}, u32[]{:S(2)}, u32[]{:S(2)}) collective-permute-start(bf16[512,256]{1,0:T(8,128)(2,1)S(1)} %get-tuple-element.33), channel_id=1, source_target_pairs={{0,8},{4,12},{9,1},{13,5},{18,26},{22,30},{27,19},{31,23}} | collective-permute-start | bytes 786440 | tf_op jit(solution)/shard_map/cond/branch_0_fun/ppermute | solution.py:355
  14.0 1.3 %collective-permute-start.5 = (bf16[512,256]{1,0:T(8,128)(2,1)S(1)}, bf16[512,256]{1,0:T(8,128)(2,1)S(1)}, u32[]{:S(2)}, u32[]{:S(2)}) collective-permute-start(bf16[512,256]{1,0:T(8,128)(2,1)S(1)} %get-tuple-element.34), channel_id=1, source_target_pairs={{0,16},{4,20},{9,25},{13,29},{18,2},{22,6},{27,11},{31,15}} | collective-permute-start | bytes 786440 | tf_op jit(solution)/shard_map/cond/branch_0_fun/ppermute | solution.py:355
  15.3 11.1 %collective-permute-done.6.yb2 = bf16[256,256]{1,0:T(8,128)(2,1)S(1)} collective-permute-done((bf16[256,256]{1,0:T(8,128)(2,1)S(1)}, bf16[256,256]{1,0:T(8,128)(2,1)S(1)}, u32[]{:S(2)}, u32[]{:S(2)}) %collective-permute-start.6) | collective-permute-done | bytes 131104 | tf_op jit(solution)/shard_map/cond/branch_0_fun/ppermute | solution.py:355
  26.4 1.3 %collective-permute-start.9 = (bf16[768,256]{1,0:T(8,128)(2,1)S(1)}, bf16[768,256]{1,0:T(8,128)(2,1)S(1)}, u32[]{:S(2)}, u32[]{:S(2)}) collective-permute-start(bf16[768,256]{1,0:T(8,128)(2,1)S(1)} %get-tuple-element.31.b), channel_id=1, source_target_pairs={{0,8},{4,12},{9,1},{13,5},{18,26},{22,30},{27,19},{31,23}} | collective-permute-start | bytes 1179656 | tf_op jit(solution)/shard_map/cond/branch_0_fun/ppermute | solution.py:355
  27.7 0.7 collective-permute-start.8
  28.4 0.7 collective-permute-start.2
  29.1 1.9 %collective-permute-done.5.yb1 = bf16[512,256]{1,0:T(8,128)(2,1)S(1)} collective-permute-done((bf16[512,256]{1,0:T(8,128)(2,1)S(1)}, bf16[512,256]{1,0:T(8,128)(2,1)S(1)}, u32[]{:S(2)}, u32[]{:S(2)}) %collective-permute-start.5) | collective-permute-done | bytes 262176 | tf_op jit(solution)/shard_map/cond/branch_0_fun/ppermute | solution.py:355
  31.0 0.7 collective-permute-start.3
  31.7 0.7 collective-permute-start.7
  32.4 2.2 %collective-permute-done.9.xb = bf16[768,256]{1,0:T(8,128)(2,1)S(1)} collective-permute-done((bf16[768,256]{1,0:T(8,128)(2,1)S(1)}, bf16[768,256]{1,0:T(8,128)(2,1)S(1)}, u32[]{:S(2)}, u32[]{:S(2)}) %collective-permute-start.9) | collective-permute-done | bytes 393248 | tf_op jit(solution)/shard_map/cond/branch_0_fun/ppermute | solution.py:355
  34.7 0.2 branch_0_fun.33.own
  34.9 2.7 %branch_0_fun.36.left = bf16[512,3584]{1,0:T(8,128)(2,1)S(1)} custom-call(s32[7]{0:T(128)S(1)} %get-tuple-element.26.rows, s32[14]{0:T(128)S(1)} %get-tuple-element.28.cols, bf16[2304,4608]{1,0:T(8,128)(2,1)} %get-tuple-element.121.a), custom_call_target="tpu_custom_call" | custom-call | tf_op jit(solution)/shard_map/cond/branch_0_fun/pallas_call | solution.py:389
  37.7 2.7 %branch_0_fun.35.left = bf16[512,3584]{1,0:T(8,128)(2,1)S(1)} custom-call(s32[7]{0:T(128)S(1)} %get-tuple-element.26.rows, s32[14]{0:T(128)S(1)} %get-tuple-element.28.cols, bf16[2304,4608]{1,0:T(8,128)(2,1)} %get-tuple-element.121.a), custom_call_target="tpu_custom_call" | custom-call | tf_op jit(solution)/shard_map/cond/branch_0_fun/pallas_call | solution.py:389
  40.4 2.7 %branch_0_fun.34.left = bf16[512,3584]{1,0:T(8,128)(2,1)S(1)} custom-call(s32[7]{0:T(128)S(1)} %get-tuple-element.26.rows, s32[14]{0:T(128)S(1)} %get-tuple-element.28.cols, bf16[2304,4608]{1,0:T(8,128)(2,1)} %get-tuple-element.121.a), custom_call_target="tpu_custom_call" | custom-call | tf_op jit(solution)/shard_map/cond/branch_0_fun/pallas_call | solution.py:389
  43.2 1.8 %branch_0_fun.37 = (f32[512,256]{1,0:T(8,128)S(1)}, s16[528,256]{1,0:T(8,128)(2,1)S(1)}, f32[256,256]{1,0:T(8,128)S(1)}) custom-call(bf16[512,3584]{1,0:T(8,128)(2,1)S(1)} %branch_0_fun.36.left, bf16[1792,256]{1,0:T(8,128)(2,1)S(1)} %branch_0_fun.33.own, bf16[1792,256]{1,0:T(8,128)(2,1)S(1)} %collective-permute-done.10.other, ...), custom_call_target="tpu_custom_call" | custom-call | tf_op jit(solution)/shard_map/cond/branch_0_fun/pallas_call | solution.py:451
  45.0 5.4 %collective-permute-start.20 = (s16[528,256]{1,0:T(8,128)(2,1)S(1)}, s16[528,256]{1,0:T(8,128)(2,1)S(1)}, u32[]{:S(2)}, u32[]{:S(2)}) collective-permute-start(s16[528,256]{1,0:T(8,128)(2,1)S(1)} %get-tuple-element.46.mine), channel_id=1, source_target_pairs={{0,1},{3,2},{4,5},{7,6},{8,9},{11,10},{12,13},{15,14},{16,17},{19,... | collective-permute-start | bytes 811016 | tf_op jit(solution)/shard_map/cond/branch_0_fun/ppermute | solution.py:355
  50.4 1.8 %branch_0_fun.38 = (f32[512,256]{1,0:T(8,128)S(1)}, s16[528,256]{1,0:T(8,128)(2,1)S(1)}, f32[256,256]{1,0:T(8,128)S(1)}) custom-call(bf16[512,3584]{1,0:T(8,128)(2,1)S(1)} %branch_0_fun.35.left, bf16[1792,256]{1,0:T(8,128)(2,1)S(1)} %branch_0_fun.33.own, bf16[1792,256]{1,0:T(8,128)(2,1)S(1)} %collective-permute-done.10.other, ...), custom_call_target="tpu_custom_call" | custom-call | tf_op jit(solution)/shard_map/cond/branch_0_fun/pallas_call | solution.py:451
  52.2 1.3 %collective-permute-start.17 = (s16[528,256]{1,0:T(8,128)(2,1)S(1)}, s16[528,256]{1,0:T(8,128)(2,1)S(1)}, u32[]{:S(2)}, u32[]{:S(2)}) collective-permute-start(s16[528,256]{1,0:T(8,128)(2,1)S(1)} %get-tuple-element.44.mine), channel_id=1, source_target_pairs={{0,1},{3,2},{4,5},{7,6},{8,9},{11,10},{12,13},{15,14},{16,17},{19,... | collective-permute-start | bytes 811016 | tf_op jit(solution)/shard_map/cond/branch_0_fun/ppermute | solution.py:355
  53.5 1.8 %branch_0_fun.39 = (f32[512,256]{1,0:T(8,128)S(1)}, s16[528,256]{1,0:T(8,128)(2,1)S(1)}, f32[256,256]{1,0:T(8,128)S(1)}) custom-call(bf16[512,3584]{1,0:T(8,128)(2,1)S(1)} %branch_0_fun.34.left, bf16[1792,256]{1,0:T(8,128)(2,1)S(1)} %branch_0_fun.33.own, bf16[1792,256]{1,0:T(8,128)(2,1)S(1)} %collective-permute-done.10.other, ...), custom_call_target="tpu_custom_call" | custom-call | tf_op jit(solution)/shard_map/cond/branch_0_fun/pallas_call | solution.py:451
  55.3 1.3 %collective-permute-start.14 = (s16[528,256]{1,0:T(8,128)(2,1)S(1)}, s16[528,256]{1,0:T(8,128)(2,1)S(1)}, u32[]{:S(2)}, u32[]{:S(2)}) collective-permute-start(s16[528,256]{1,0:T(8,128)(2,1)S(1)} %get-tuple-element.42.mine), channel_id=1, source_target_pairs={{0,1},{3,2},{4,5},{7,6},{8,9},{11,10},{12,13},{15,14},{16,17},{19,... | collective-permute-start | bytes 811016 | tf_op jit(solution)/shard_map/cond/branch_0_fun/ppermute | solution.py:355
  56.6 2.1 %branch_0_fun.32.left = bf16[256,3584]{1,0:T(8,128)(2,1)S(1)} custom-call(s32[7]{0:T(128)S(1)} %get-tuple-element.26.rows, s32[14]{0:T(128)S(1)} %get-tuple-element.28.cols, bf16[2304,4608]{1,0:T(8,128)(2,1)} %get-tuple-element.121.a), custom_call_target="tpu_custom_call" | custom-call | tf_op jit(solution)/shard_map/cond/branch_0_fun/pallas_call | solution.py:389
  58.8 1.1 branch_0_fun.40
  59.9 0.5 collective-permute-start.23
  60.4 1.0 collective-permute-done.23.y
  61.5 0.2 branch_0_fun.47.mine
  61.7 0.7 collective-permute-start.21
  62.4 0.7 collective-permute-done.17.came
  63.0 0.2 branch_0_fun.45.mine
  63.2 0.7 collective-permute-start.18
  63.9 4.6 %collective-permute-done.14.came = s16[528,256]{1,0:T(8,128)(2,1)S(1)} collective-permute-done((s16[528,256]{1,0:T(8,128)(2,1)S(1)}, s16[528,256]{1,0:T(8,128)(2,1)S(1)}, u32[]{:S(2)}, u32[]{:S(2)}) %collective-permute-start.14) | collective-permute-done | bytes 270368 | tf_op jit(solution)/shard_map/cond/branch_0_fun/ppermute | solution.py:355
  68.5 0.2 branch_0_fun.43.mine
  68.7 0.7 collective-permute-start.15
  69.4 12.8 %collective-permute-start.11 = (s16[272,256]{1,0:T(8,128)(2,1)S(1)}, s16[272,256]{1,0:T(8,128)(2,1)S(1)}, u32[]{:S(2)}, u32[]{:S(2)}) collective-permute-start(s16[272,256]{1,0:T(8,128)(2,1)S(1)} %get-tuple-element.40.mine), channel_id=1, source_target_pairs={{0,1},{3,2},{4,5},{7,6},{8,9},{11,10},{12,13},{15,14},{16,17},{19,... | collective-permute-start | bytes 417800 | tf_op jit(solution)/shard_map/cond/branch_0_fun/ppermute | solution.py:355
  82.3 5.0 %collective-permute-done.25.y = f32[256,128]{1,0:T(8,128)S(1)} collective-permute-done((f32[256,128]{1,0:T(8,128)S(1)}, f32[256,128]{1,0:T(8,128)S(1)}, u32[]{:S(2)}, u32[]{:S(2)}) %collective-permute-start.25) | collective-permute-done | bytes 131104 | tf_op jit(solution)/shard_map/cond/branch_0_fun/ppermute | solution.py:355
  87.3 0.1 branch_0_fun.57.mine
  87.4 1.6 %collective-permute-start.26 = (s16[272,128]{1,0:T(8,128)(2,1)S(1)}, s16[272,128]{1,0:T(8,128)(2,1)S(1)}, u32[]{:S(2)}, u32[]{:S(2)}) collective-permute-start(s16[272,128]{1,0:T(8,128)(2,1)S(1)} %branch_0_fun.57.mine), channel_id=1, source_target_pairs={{0,1},{3,2},{4,5},{7,6},{8,9},{11,10},{12,13},{15,14},{16,17},{19,... | collective-permute-start | bytes 208904 | tf_op jit(solution)/shard_map/cond/branch_0_fun/ppermute | solution.py:355
  89.0 0.1 branch_0_fun.41.mine
  89.2 0.7 collective-permute-start.12
  89.8 0.3 branch_0_fun.48.total
  90.1 1.3 %collective-permute-start.22 = (s16[528,256]{1,0:T(8,128)(2,1)S(1)}, s16[528,256]{1,0:T(8,128)(2,1)S(1)}, u32[]{:S(2)}, u32[]{:S(2)}) collective-permute-start(s16[528,256]{1,0:T(8,128)(2,1)S(1)} %branch_0_fun.48.total), channel_id=1, source_target_pairs={{1,0},{2,3},{5,4},{6,7},{9,8},{10,11},{13,12},{14,15},{17,16},{18,... | collective-permute-start | bytes 811016 | tf_op jit(solution)/shard_map/cond/branch_0_fun/ppermute | solution.py:355
  91.4 0.3 branch_0_fun.46.total
  91.7 1.3 %collective-permute-start.19 = (s16[528,256]{1,0:T(8,128)(2,1)S(1)}, s16[528,256]{1,0:T(8,128)(2,1)S(1)}, u32[]{:S(2)}, u32[]{:S(2)}) collective-permute-start(s16[528,256]{1,0:T(8,128)(2,1)S(1)} %branch_0_fun.46.total), channel_id=1, source_target_pairs={{1,0},{2,3},{5,4},{6,7},{9,8},{10,11},{13,12},{14,15},{17,16},{18,... | collective-permute-start | bytes 811016 | tf_op jit(solution)/shard_map/cond/branch_0_fun/ppermute | solution.py:355
  93.0 0.3 branch_0_fun.44.total
  93.3 1.3 %collective-permute-start.16 = (s16[528,256]{1,0:T(8,128)(2,1)S(1)}, s16[528,256]{1,0:T(8,128)(2,1)S(1)}, u32[]{:S(2)}, u32[]{:S(2)}) collective-permute-start(s16[528,256]{1,0:T(8,128)(2,1)S(1)} %branch_0_fun.44.total), channel_id=1, source_target_pairs={{1,0},{2,3},{5,4},{6,7},{9,8},{10,11},{13,12},{14,15},{17,16},{18,... | collective-permute-start | bytes 811016 | tf_op jit(solution)/shard_map/cond/branch_0_fun/ppermute | solution.py:355
  94.6 0.1 branch_0_fun.58.mine
  94.7 0.7 collective-permute-start.27
  95.4 0.1 branch_0_fun.59.total
  95.5 1.3 %collective-permute-start.28 = (s16[272,128]{1,0:T(8,128)(2,1)S(1)}, s16[272,128]{1,0:T(8,128)(2,1)S(1)}, u32[]{:S(2)}, u32[]{:S(2)}) collective-permute-start(s16[272,128]{1,0:T(8,128)(2,1)S(1)} %branch_0_fun.59.total), channel_id=1, source_target_pairs={{1,0},{2,3},{5,4},{6,7},{9,8},{10,11},{13,12},{14,15},{17,16},{18,... | collective-permute-start | bytes 208904 | tf_op jit(solution)/shard_map/cond/branch_0_fun/ppermute | solution.py:355
  96.8 0.2 branch_0_fun.42.total
  97.0 1.3 %collective-permute-start.13 = (s16[272,256]{1,0:T(8,128)(2,1)S(1)}, s16[272,256]{1,0:T(8,128)(2,1)S(1)}, u32[]{:S(2)}, u32[]{:S(2)}) collective-permute-start(s16[272,256]{1,0:T(8,128)(2,1)S(1)} %branch_0_fun.42.total), channel_id=1, source_target_pairs={{1,0},{2,3},{5,4},{6,7},{9,8},{10,11},{13,12},{14,15},{17,16},{18,... | collective-permute-start | bytes 417800 | tf_op jit(solution)/shard_map/cond/branch_0_fun/ppermute | solution.py:355
  98.3 15.4 %collective-permute-done.28.came = s16[272,128]{1,0:T(8,128)(2,1)S(1)} collective-permute-done((s16[272,128]{1,0:T(8,128)(2,1)S(1)}, s16[272,128]{1,0:T(8,128)(2,1)S(1)}, u32[]{:S(2)}, u32[]{:S(2)}) %collective-permute-start.28) | collective-permute-done | bytes 69664 | tf_op jit(solution)/shard_map/cond/branch_0_fun/ppermute | solution.py:355
  113.8 1.2 %collective-permute-done.29.other = s16[272,128]{1,0:T(8,128)(2,1)S(1)} collective-permute-done((s16[272,128]{1,0:T(8,128)(2,1)S(1)}, s16[272,128]{1,0:T(8,128)(2,1)S(1)}, u32[]{:S(2)}, u32[]{:S(2)}) %collective-permute-start.29) | collective-permute-done | bytes 69664 | tf_op jit(solution)/shard_map/cond/branch_0_fun/ppermute | solution.py:355
  115.1 0.8 branch_0_fun.61
  115.8 1.0 branch_0_fun.49.refs_0_
  116.9 0.8 branch_0_fun.50.refs_0_
  117.8 0.9 branch_0_fun.51.refs_0_
  118.6 0.7 branch_0_fun.52
  119.4 1.4 %copy-done = f32[2304,256]{1,0:T(8,128)} copy-done((f32[2304,256]{1,0:T(8,128)}, f32[2304,256]{1,0:T(8,128)S(1)}, u32[]{:S(2)}) %copy-start) | copy-done | bytes 2359320 | tf_op jit(solution)/shard_map/cond
  (35 shorter events, 0.5 us)
Async XLA Ops:
  5.3 22.4 %collective-permute-start = (bf16[512,256]{1,0:T(8,128)(2,1)S(1)}, bf16[512,256]{1,0:T(8,128)(2,1)S(1)}, u32[]{:S(2)}, u32[]{:S(2)}) collective-permute-start(bf16[512,256]{1,0:T(8,128)(2,1)S(1)} %get-tuple-element.32), channel_id=1, source_target_pairs={{0,8},{4,12},{9,1},{13,5},{18,26},{22,30},{27,19},{31,23}} | collective-permute-start | bytes 786440 | tf_op jit(solution)/shard_map/cond/branch_0_fun/ppermute | solution.py:355
  10.0 24.6 %collective-permute-start.4 = (bf16[1024,256]{1,0:T(8,128)(2,1)S(1)}, bf16[1024,256]{1,0:T(8,128)(2,1)S(1)}, u32[]{:S(2)}, u32[]{:S(2)}) collective-permute-start(bf16[1024,256]{1,0:T(8,128)(2,1)S(1)} %get-tuple-element.30.a), channel_id=1, source_target_pairs={{0,16},{4,20},{9,25},{13,29},{18,2},{22,6},{27,11},{31,15}} | collective-permute-start | bytes 1572872 | tf_op jit(solution)/shard_map/cond/branch_0_fun/ppermute | solution.py:355
  11.3 15.1 %collective-permute-start.6 = (bf16[256,256]{1,0:T(8,128)(2,1)S(1)}, bf16[256,256]{1,0:T(8,128)(2,1)S(1)}, u32[]{:S(2)}, u32[]{:S(2)}) collective-permute-start(bf16[256,256]{1,0:T(8,128)(2,1)S(1)} %get-tuple-element.35), channel_id=1, source_target_pairs={{0,16},{4,20},{9,25},{13,29},{18,2},{22,6},{27,11},{31,15}} | collective-permute-start | bytes 393224 | tf_op jit(solution)/shard_map/cond/branch_0_fun/ppermute | solution.py:355
  12.6 15.8 %collective-permute-start.1 = (bf16[512,256]{1,0:T(8,128)(2,1)S(1)}, bf16[512,256]{1,0:T(8,128)(2,1)S(1)}, u32[]{:S(2)}, u32[]{:S(2)}) collective-permute-start(bf16[512,256]{1,0:T(8,128)(2,1)S(1)} %get-tuple-element.33), channel_id=1, source_target_pairs={{0,8},{4,12},{9,1},{13,5},{18,26},{22,30},{27,19},{31,23}} | collective-permute-start | bytes 786440 | tf_op jit(solution)/shard_map/cond/branch_0_fun/ppermute | solution.py:355
  14.0 17.1 %collective-permute-start.5 = (bf16[512,256]{1,0:T(8,128)(2,1)S(1)}, bf16[512,256]{1,0:T(8,128)(2,1)S(1)}, u32[]{:S(2)}, u32[]{:S(2)}) collective-permute-start(bf16[512,256]{1,0:T(8,128)(2,1)S(1)} %get-tuple-element.34), channel_id=1, source_target_pairs={{0,16},{4,20},{9,25},{13,29},{18,2},{22,6},{27,11},{31,15}} | collective-permute-start | bytes 786440 | tf_op jit(solution)/shard_map/cond/branch_0_fun/ppermute | solution.py:355
  26.4 8.2 %collective-permute-start.9 = (bf16[768,256]{1,0:T(8,128)(2,1)S(1)}, bf16[768,256]{1,0:T(8,128)(2,1)S(1)}, u32[]{:S(2)}, u32[]{:S(2)}) collective-permute-start(bf16[768,256]{1,0:T(8,128)(2,1)S(1)} %get-tuple-element.31.b), channel_id=1, source_target_pairs={{0,8},{4,12},{9,1},{13,5},{18,26},{22,30},{27,19},{31,23}} | collective-permute-start | bytes 1179656 | tf_op jit(solution)/shard_map/cond/branch_0_fun/ppermute | solution.py:355
  27.7 4.0 %collective-permute-start.8 = (bf16[256,256]{1,0:T(8,128)(2,1)S(1)}, bf16[256,256]{1,0:T(8,128)(2,1)S(1)}, u32[]{:S(2)}, u32[]{:S(2)}) collective-permute-start(bf16[256,256]{1,0:T(8,128)(2,1)S(1)} %collective-permute-done.6.yb2), channel_id=1, source_target_pairs={{2,10},{6,14},{11,3},{15,7},{16,24},{20,28},{25,17},{29,21}} | collective-permute-start | bytes 393224 | tf_op jit(solution)/shard_map/cond/branch_0_fun/ppermute | solution.py:355
  28.4 6.2 %collective-permute-start.2 = (bf16[512,256]{1,0:T(8,128)(2,1)S(1)}, bf16[512,256]{1,0:T(8,128)(2,1)S(1)}, u32[]{:S(2)}, u32[]{:S(2)}) collective-permute-start(bf16[512,256]{1,0:T(8,128)(2,1)S(1)} %collective-permute-done.xa1), channel_id=1, source_target_pairs={{1,17},{5,21},{8,24},{12,28},{19,3},{23,7},{26,10},{30,14}} | collective-permute-start | bytes 786440 | tf_op jit(solution)/shard_map/cond/branch_0_fun/ppermute | solution.py:355
  31.0 3.6 %collective-permute-start.3 = (bf16[512,256]{1,0:T(8,128)(2,1)S(1)}, bf16[512,256]{1,0:T(8,128)(2,1)S(1)}, u32[]{:S(2)}, u32[]{:S(2)}) collective-permute-start(bf16[512,256]{1,0:T(8,128)(2,1)S(1)} %collective-permute-done.1.xa2), channel_id=1, source_target_pairs={{1,17},{5,21},{8,24},{12,28},{19,3},{23,7},{26,10},{30,14}} | collective-permute-start | bytes 786440 | tf_op jit(solution)/shard_map/cond/branch_0_fun/ppermute | solution.py:355
  31.7 2.9 %collective-permute-start.7 = (bf16[512,256]{1,0:T(8,128)(2,1)S(1)}, bf16[512,256]{1,0:T(8,128)(2,1)S(1)}, u32[]{:S(2)}, u32[]{:S(2)}) collective-permute-start(bf16[512,256]{1,0:T(8,128)(2,1)S(1)} %collective-permute-done.5.yb1), channel_id=1, source_target_pairs={{2,10},{6,14},{11,3},{15,7},{16,24},{20,28},{25,17},{29,21}} | collective-permute-start | bytes 786440 | tf_op jit(solution)/shard_map/cond/branch_0_fun/ppermute | solution.py:355
  34.9 8.3 %collective-permute-start.10 = (bf16[1792,256]{1,0:T(8,128)(2,1)S(1)}, bf16[1792,256]{1,0:T(8,128)(2,1)S(1)}, u32[]{:S(2)}, u32[]{:S(2)}) collective-permute-start(bf16[1792,256]{1,0:T(8,128)(2,1)S(1)} %branch_0_fun.33.own), channel_id=1, source_target_pairs={{0,4},{1,5},{2,6},{3,7},{4,0},{5,1},{6,2},{7,3},{8,12},{9,13},{10,... | collective-permute-start | bytes 2752520 | tf_op jit(solution)/shard_map/cond/branch_0_fun/ppermute | solution.py:355
  45.0 16.5 %collective-permute-start.20 = (s16[528,256]{1,0:T(8,128)(2,1)S(1)}, s16[528,256]{1,0:T(8,128)(2,1)S(1)}, u32[]{:S(2)}, u32[]{:S(2)}) collective-permute-start(s16[528,256]{1,0:T(8,128)(2,1)S(1)} %get-tuple-element.46.mine), channel_id=1, source_target_pairs={{0,1},{3,2},{4,5},{7,6},{8,9},{11,10},{12,13},{15,14},{16,17},{19,... | collective-permute-start | bytes 811016 | tf_op jit(solution)/shard_map/cond/branch_0_fun/ppermute | solution.py:355
  52.2 10.8 %collective-permute-start.17 = (s16[528,256]{1,0:T(8,128)(2,1)S(1)}, s16[528,256]{1,0:T(8,128)(2,1)S(1)}, u32[]{:S(2)}, u32[]{:S(2)}) collective-permute-start(s16[528,256]{1,0:T(8,128)(2,1)S(1)} %get-tuple-element.44.mine), channel_id=1, source_target_pairs={{0,1},{3,2},{4,5},{7,6},{8,9},{11,10},{12,13},{15,14},{16,17},{19,... | collective-permute-start | bytes 811016 | tf_op jit(solution)/shard_map/cond/branch_0_fun/ppermute | solution.py:355
  55.3 13.2 %collective-permute-start.14 = (s16[528,256]{1,0:T(8,128)(2,1)S(1)}, s16[528,256]{1,0:T(8,128)(2,1)S(1)}, u32[]{:S(2)}, u32[]{:S(2)}) collective-permute-start(s16[528,256]{1,0:T(8,128)(2,1)S(1)} %get-tuple-element.42.mine), channel_id=1, source_target_pairs={{0,1},{3,2},{4,5},{7,6},{8,9},{11,10},{12,13},{15,14},{16,17},{19,... | collective-permute-start | bytes 811016 | tf_op jit(solution)/shard_map/cond/branch_0_fun/ppermute | solution.py:355
  59.9 1.4 %collective-permute-start.23 = (f32[256,128]{1,0:T(8,128)S(1)}, f32[256,128]{1,0:T(8,128)S(1)}, u32[]{:S(2)}, u32[]{:S(2)}) collective-permute-start(f32[256,128]{1,0:T(8,128)S(1)} %get-tuple-element.50), channel_id=1, source_target_pairs={{0,4},{1,5},{2,6},{3,7},{4,0},{5,1},{6,2},{7,3},{8,12},{9,13},{10,... | collective-permute-start | bytes 393224 | tf_op jit(solution)/shard_map/cond/branch_0_fun/ppermute | solution.py:355
  61.4 20.8 %collective-permute-start.24 = (f32[256,128]{1,0:T(8,128)S(1)}, f32[256,128]{1,0:T(8,128)S(1)}, u32[]{:S(2)}, u32[]{:S(2)}) collective-permute-start(f32[256,128]{1,0:T(8,128)S(1)} %branch_0_fun.54.x), channel_id=1, source_target_pairs={{0,8},{1,9},{2,10},{3,11},{4,12},{5,13},{6,14},{7,15},{8,0},{9,1},... | collective-permute-start | bytes 393224 | tf_op jit(solution)/shard_map/cond/branch_0_fun/ppermute | solution.py:355
  61.7 28.2 %collective-permute-start.21 = (s16[528,256]{1,0:T(8,128)(2,1)S(1)}, s16[528,256]{1,0:T(8,128)(2,1)S(1)}, u32[]{:S(2)}, u32[]{:S(2)}) collective-permute-start(s16[528,256]{1,0:T(8,128)(2,1)S(1)} %branch_0_fun.47.mine), channel_id=1, source_target_pairs={{1,2},{2,1},{5,6},{6,5},{9,10},{10,9},{13,14},{14,13},{17,18},{18,... | collective-permute-start | bytes 811016 | tf_op jit(solution)/shard_map/cond/branch_0_fun/ppermute | solution.py:355
  63.2 28.2 %collective-permute-start.18 = (s16[528,256]{1,0:T(8,128)(2,1)S(1)}, s16[528,256]{1,0:T(8,128)(2,1)S(1)}, u32[]{:S(2)}, u32[]{:S(2)}) collective-permute-start(s16[528,256]{1,0:T(8,128)(2,1)S(1)} %branch_0_fun.45.mine), channel_id=1, source_target_pairs={{1,2},{2,1},{5,6},{6,5},{9,10},{10,9},{13,14},{14,13},{17,18},{18,... | collective-permute-start | bytes 811016 | tf_op jit(solution)/shard_map/cond/branch_0_fun/ppermute | solution.py:355
  68.7 24.3 %collective-permute-start.15 = (s16[528,256]{1,0:T(8,128)(2,1)S(1)}, s16[528,256]{1,0:T(8,128)(2,1)S(1)}, u32[]{:S(2)}, u32[]{:S(2)}) collective-permute-start(s16[528,256]{1,0:T(8,128)(2,1)S(1)} %branch_0_fun.43.mine), channel_id=1, source_target_pairs={{1,2},{2,1},{5,6},{6,5},{9,10},{10,9},{13,14},{14,13},{17,18},{18,... | collective-permute-start | bytes 811016 | tf_op jit(solution)/shard_map/cond/branch_0_fun/ppermute | solution.py:355
  69.4 19.6 %collective-permute-start.11 = (s16[272,256]{1,0:T(8,128)(2,1)S(1)}, s16[272,256]{1,0:T(8,128)(2,1)S(1)}, u32[]{:S(2)}, u32[]{:S(2)}) collective-permute-start(s16[272,256]{1,0:T(8,128)(2,1)S(1)} %get-tuple-element.40.mine), channel_id=1, source_target_pairs={{0,1},{3,2},{4,5},{7,6},{8,9},{11,10},{12,13},{15,14},{16,17},{19,... | collective-permute-start | bytes 417800 | tf_op jit(solution)/shard_map/cond/branch_0_fun/ppermute | solution.py:355
  82.3 32.8 %copy-start.3 = (f32[256,256]{1,0:T(8,128)S(1)}, f32[256,256]{1,0:T(8,128)}, u32[]{:S(2)}) copy-start(f32[256,256]{1,0:T(8,128)} %get-tuple-element.124.base) | copy-start | bytes 786436 | tf_op jit(solution)/shard_map/cond
  82.3 5.1 %collective-permute-start.25 = (f32[256,128]{1,0:T(8,128)S(1)}, f32[256,128]{1,0:T(8,128)S(1)}, u32[]{:S(2)}, u32[]{:S(2)}) collective-permute-start(f32[256,128]{1,0:T(8,128)S(1)} %branch_0_fun.55.x), channel_id=1, source_target_pairs={{0,16},{1,17},{2,18},{3,19},{4,20},{5,21},{6,22},{7,23},{8,24},{9,... | collective-permute-start | bytes 393224 | tf_op jit(solution)/shard_map/cond/branch_0_fun/ppermute | solution.py:355
  87.4 7.2 %collective-permute-start.26 = (s16[272,128]{1,0:T(8,128)(2,1)S(1)}, s16[272,128]{1,0:T(8,128)(2,1)S(1)}, u32[]{:S(2)}, u32[]{:S(2)}) collective-permute-start(s16[272,128]{1,0:T(8,128)(2,1)S(1)} %branch_0_fun.57.mine), channel_id=1, source_target_pairs={{0,1},{3,2},{4,5},{7,6},{8,9},{11,10},{12,13},{15,14},{16,17},{19,... | collective-permute-start | bytes 208904 | tf_op jit(solution)/shard_map/cond/branch_0_fun/ppermute | solution.py:355
  89.0 26.8 %copy-start.6 = (s32[72]{0:T(128)S(1)}, s32[72]{0:T(128)}, u32[]{:S(2)}) copy-start(s32[72]{0:T(128)} %get-tuple-element.24.live) | copy-start | bytes 868 | tf_op jit(solution)/shard_map/cond
  89.2 7.7 %collective-permute-start.12 = (s16[272,256]{1,0:T(8,128)(2,1)S(1)}, s16[272,256]{1,0:T(8,128)(2,1)S(1)}, u32[]{:S(2)}, u32[]{:S(2)}) collective-permute-start(s16[272,256]{1,0:T(8,128)(2,1)S(1)} %branch_0_fun.41.mine), channel_id=1, source_target_pairs={{1,2},{2,1},{5,6},{6,5},{9,10},{10,9},{13,14},{14,13},{17,18},{18,... | collective-permute-start | bytes 417800 | tf_op jit(solution)/shard_map/cond/branch_0_fun/ppermute | solution.py:355
  90.1 25.7 %collective-permute-start.22 = (s16[528,256]{1,0:T(8,128)(2,1)S(1)}, s16[528,256]{1,0:T(8,128)(2,1)S(1)}, u32[]{:S(2)}, u32[]{:S(2)}) collective-permute-start(s16[528,256]{1,0:T(8,128)(2,1)S(1)} %branch_0_fun.48.total), channel_id=1, source_target_pairs={{1,0},{2,3},{5,4},{6,7},{9,8},{10,11},{13,12},{14,15},{17,16},{18,... | collective-permute-start | bytes 811016 | tf_op jit(solution)/shard_map/cond/branch_0_fun/ppermute | solution.py:355
  91.7 25.1 %collective-permute-start.19 = (s16[528,256]{1,0:T(8,128)(2,1)S(1)}, s16[528,256]{1,0:T(8,128)(2,1)S(1)}, u32[]{:S(2)}, u32[]{:S(2)}) collective-permute-start(s16[528,256]{1,0:T(8,128)(2,1)S(1)} %branch_0_fun.46.total), channel_id=1, source_target_pairs={{1,0},{2,3},{5,4},{6,7},{9,8},{10,11},{13,12},{14,15},{17,16},{18,... | collective-permute-start | bytes 811016 | tf_op jit(solution)/shard_map/cond/branch_0_fun/ppermute | solution.py:355
  93.3 24.4 %collective-permute-start.16 = (s16[528,256]{1,0:T(8,128)(2,1)S(1)}, s16[528,256]{1,0:T(8,128)(2,1)S(1)}, u32[]{:S(2)}, u32[]{:S(2)}) collective-permute-start(s16[528,256]{1,0:T(8,128)(2,1)S(1)} %branch_0_fun.44.total), channel_id=1, source_target_pairs={{1,0},{2,3},{5,4},{6,7},{9,8},{10,11},{13,12},{14,15},{17,16},{18,... | collective-permute-start | bytes 811016 | tf_op jit(solution)/shard_map/cond/branch_0_fun/ppermute | solution.py:355
  94.7 0.7 collective-permute-start.27
  95.5 18.2 %collective-permute-start.28 = (s16[272,128]{1,0:T(8,128)(2,1)S(1)}, s16[272,128]{1,0:T(8,128)(2,1)S(1)}, u32[]{:S(2)}, u32[]{:S(2)}) collective-permute-start(s16[272,128]{1,0:T(8,128)(2,1)S(1)} %branch_0_fun.59.total), channel_id=1, source_target_pairs={{1,0},{2,3},{5,4},{6,7},{9,8},{10,11},{13,12},{14,15},{17,16},{18,... | collective-permute-start | bytes 208904 | tf_op jit(solution)/shard_map/cond/branch_0_fun/ppermute | solution.py:355
  97.0 21.6 %collective-permute-start.13 = (s16[272,256]{1,0:T(8,128)(2,1)S(1)}, s16[272,256]{1,0:T(8,128)(2,1)S(1)}, u32[]{:S(2)}, u32[]{:S(2)}) collective-permute-start(s16[272,256]{1,0:T(8,128)(2,1)S(1)} %branch_0_fun.42.total), channel_id=1, source_target_pairs={{1,0},{2,3},{5,4},{6,7},{9,8},{10,11},{13,12},{14,15},{17,16},{18,... | collective-permute-start | bytes 417800 | tf_op jit(solution)/shard_map/cond/branch_0_fun/ppermute | solution.py:355
  113.7 1.3 %collective-permute-start.29 = (s16[272,128]{1,0:T(8,128)(2,1)S(1)}, s16[272,128]{1,0:T(8,128)(2,1)S(1)}, u32[]{:S(2)}, u32[]{:S(2)}) collective-permute-start(s16[272,128]{1,0:T(8,128)(2,1)S(1)} %branch_0_fun.60.mine), channel_id=1, source_target_pairs={{0,4},{1,5},{2,6},{3,7},{4,0},{5,1},{6,2},{7,3},{8,12},{9,13},{10,... | collective-permute-start | bytes 208904 | tf_op jit(solution)/shard_map/cond/branch_0_fun/ppermute | solution.py:355
  119.4 1.4 %copy-start = (f32[2304,256]{1,0:T(8,128)}, f32[2304,256]{1,0:T(8,128)S(1)}, u32[]{:S(2)}) copy-start(f32[2304,256]{1,0:T(8,128)S(1)} %branch_0_fun.52) | copy-start | bytes 7077892 | tf_op jit(solution)/shard_map/cond

commit v2 on v1

--- a/solution.py
+++ b/solution.py
@@ -11,7 +11,7 @@
 AXES = ("prow", "pcol")
 SMALLEST = 7
 SCRATCH = 8 << 20
-ROWS = 64
+ROWS = 32
 TAIL = 16
 STEPS = 64.0
 TOP = 32760.0
@@ -199,13 +199,25 @@
                 inner += e.shape[0]
 
 
+def early_kernel(left, own, part, *, size):
+    def one(i, _):
+        at = pl.ds(pl.multiple_of(i * size, size), size)
+        part[at, :] = jnp.dot(left[at, : own.shape[0]], own[...], preferred_element_type=F32)
+        return 0
+
+    lax.fori_loop(0, left.shape[0] // size, one, 0)
+
+
 def product_kernel(left, own, other, a, b, *refs, first, size):
     part, message, term = refs[-3:]
-    n_rows = own.shape[0]
+    n_rows = other.shape[0]
 
     def one(i, _):
         at = pl.ds(pl.multiple_of(i * size, size), size)
-        acc = jnp.dot(left[at, :n_rows], own[...], preferred_element_type=F32)
+        if own.dtype == F32:
+            acc = own[at, :]
+        else:
+            acc = jnp.dot(left[at, :n_rows], own[...], preferred_element_type=F32)
         part[at, :] = acc + jnp.dot(left[at, n_rows:], other[...], preferred_element_type=F32)
         return 0
 
@@ -420,6 +432,10 @@
             bit *= 2
     swap = lambda p, c: (p ^ 1, c)
     other = send(own, swap)
+    early = kernel(
+        functools.partial(early_kernel, size=size),
+        pltpu.VMEM((chunks[0] * size, width), F32), [VMEM] * 2, VMEM,
+    )(lefts[0], own)
 
     middle = n_pcol // 2
 
@@ -453,7 +469,7 @@
             [pltpu.VMEM((count * size, width), F32), pltpu.VMEM(message_shape, jnp.int16),
              pltpu.VMEM((width, width), F32)],
             [VMEM] * (5 if term is None else 6), [VMEM] * 3,
-        )(lefts[k], own, other, a, b, *(() if term is None else (term,)))
+        )(lefts[k], own if k else early, other, a, b, *(() if term is None else (term,)))
         sums.append((first, count, *sum_over_line(part, message)))
         first += count
 

time: 121 us -> 122 us (level)
  Pallas kernels: 27.4 us -> 28.9 us
  transfers between devices with their start and end apart: 30 -> 30, of which waited for: 9 -> 9; matrix products, arithmetic and copies ran while one was open for 0% -> 0% of each run, Pallas kernels for 17% -> 18%
where the time goes in v2:
time: 122 us
  starting transfers between devices  46.8 us (38%)
  waiting for transfers between devices  42.7 us (35%)
  Pallas kernels  28.9 us (24%)
  local copies, waits for them, and re-layouts  1.41 us (1%)
  between operations  1.29 us (1%)
    ppermute x30, starting transfers between devices, send(): return near(lax.ppermute(value, AXES, pairs))  46.8 us
    ppermute x30, waiting for transfers between devices, send(): return near(lax.ppermute(value, AXES, pairs))  42.7 us
    pallas_call x4, Pallas kernels, packed_step(): kernel(functools.partial(fetch_kernel, first=first, size=size), pltpu.VME...  10.3 us
    pallas_call x4, Pallas kernels, packed_step(): kernel(functools.partial(product_kernel, first=first, size=size), [pltpu....  6.33 us
    pallas_call x4, Pallas kernels, packed_step(): kernel(functools.partial(spread_kernel, first=first, size=size, per=per,...  3.69 us
    pallas_call x1, Pallas kernels, packed_step(): kernel(functools.partial(pack_kernel, ranges=ranges, n=n, per=per, ratio=...  2.75 us
  transfers between devices with their start and end apart: 30, of which 9 were waited for; matrix products, arithmetic and copies ran while one was open for 0% of the time, Pallas kernels for 18%

profile of v2, /device:TPU:0, one launch (start us, length us, event | category | flops | bytes accessed | tf_op | source)
XLA Modules:
  0.0 121.8 jit_solution(8797982796356241225)
XLA Ops:
  0.6 1.3 %shard_map.74 = s32[1]{0:T(128)} custom-call(s32[72]{0:T(128)} %live.1), custom_call_target="tpu_custom_call" | custom-call | tf_op jit(solution)/shard_map/pallas_call | solution.py:534
  2.6 119.2 %conditional.1 = (f32[2304,256]{1,0:T(8,128)}, f32[256,256]{1,0:T(8,128)}) conditional(s32[]{:T(128)} %bitcast, (s32[72]{0:T(128)}, bf16[2304,256]{1,0:T(8,128)(2,1)}, bf16[2304,4608]{1,0:T(8,128)(2,1)}, f32[256,256]{1,0:T(8,128)}) %tuple.19, (s32[72]{0:T(128)}, bf16[2304,256]{1,0:T(8,128)(2,1)}, bf16[2304,4608]{1,0:T(8,128)(2,1)}, ...), branch_computations={%region_0.0_spmd, %region_1.0_spmd, %region_2.0_spmd} | conditional | bytes 46598548 | solution.py:538
  2.6 2.8 %branch_0_fun.32 = (bf16[1024,256]{1,0:T(8,128)(2,1)S(1)}, bf16[768,256]{1,0:T(8,128)(2,1)S(1)}, bf16[512,256]{1,0:T(8,128)(2,1)S(1)}, bf16[512,256]{1,0:T(8,128...) custom-call(s32[72]{0:T(128)} %get-tuple-element.24.live, ...), custom_call_target="tpu_custom_call" | custom-call | tf_op jit(solution)/shard_map/cond/branch_0_fun/pallas_call | solution.py:380
  5.3 4.7 %collective-permute-start = (bf16[512,256]{1,0:T(8,128)(2,1)S(1)}, bf16[512,256]{1,0:T(8,128)(2,1)S(1)}, u32[]{:S(2)}, u32[]{:S(2)}) collective-permute-start(bf16[512,256]{1,0:T(8,128)(2,1)S(1)} %get-tuple-element.32), channel_id=1, source_target_pairs={{0,8},{4,12},{9,1},{13,5},{18,26},{22,30},{27,19},{31,23}} | collective-permute-start | bytes 786440 | tf_op jit(solution)/shard_map/cond/branch_0_fun/ppermute | solution.py:367
  10.0 1.3 %collective-permute-start.4 = (bf16[1024,256]{1,0:T(8,128)(2,1)S(1)}, bf16[1024,256]{1,0:T(8,128)(2,1)S(1)}, u32[]{:S(2)}, u32[]{:S(2)}) collective-permute-start(bf16[1024,256]{1,0:T(8,128)(2,1)S(1)} %get-tuple-element.30.a), channel_id=1, source_target_pairs={{0,16},{4,20},{9,25},{13,29},{18,2},{22,6},{27,11},{31,15}} | collective-permute-start | bytes 1572872 | tf_op jit(solution)/shard_map/cond/branch_0_fun/ppermute | solution.py:367
  11.3 1.3 %collective-permute-start.6 = (bf16[256,256]{1,0:T(8,128)(2,1)S(1)}, bf16[256,256]{1,0:T(8,128)(2,1)S(1)}, u32[]{:S(2)}, u32[]{:S(2)}) collective-permute-start(bf16[256,256]{1,0:T(8,128)(2,1)S(1)} %get-tuple-element.35), channel_id=1, source_target_pairs={{0,16},{4,20},{9,25},{13,29},{18,2},{22,6},{27,11},{31,15}} | collective-permute-start | bytes 393224 | tf_op jit(solution)/shard_map/cond/branch_0_fun/ppermute | solution.py:367
  12.6 1.3 %collective-permute-start.1 = (bf16[512,256]{1,0:T(8,128)(2,1)S(1)}, bf16[512,256]{1,0:T(8,128)(2,1)S(1)}, u32[]{:S(2)}, u32[]{:S(2)}) collective-permute-start(bf16[512,256]{1,0:T(8,128)(2,1)S(1)} %get-tuple-element.33), channel_id=1, source_target_pairs={{0,8},{4,12},{9,1},{13,5},{18,26},{22,30},{27,19},{31,23}} | collective-permute-start | bytes 786440 | tf_op jit(solution)/shard_map/cond/branch_0_fun/ppermute | solution.py:367
  14.0 1.3 %collective-permute-start.5 = (bf16[512,256]{1,0:T(8,128)(2,1)S(1)}, bf16[512,256]{1,0:T(8,128)(2,1)S(1)}, u32[]{:S(2)}, u32[]{:S(2)}) collective-permute-start(bf16[512,256]{1,0:T(8,128)(2,1)S(1)} %get-tuple-element.34), channel_id=1, source_target_pairs={{0,16},{4,20},{9,25},{13,29},{18,2},{22,6},{27,11},{31,15}} | collective-permute-start | bytes 786440 | tf_op jit(solution)/shard_map/cond/branch_0_fun/ppermute | solution.py:367
  15.3 11.1 %collective-permute-done.6.yb2 = bf16[256,256]{1,0:T(8,128)(2,1)S(1)} collective-permute-done((bf16[256,256]{1,0:T(8,128)(2,1)S(1)}, bf16[256,256]{1,0:T(8,128)(2,1)S(1)}, u32[]{:S(2)}, u32[]{:S(2)}) %collective-permute-start.6) | collective-permute-done | bytes 131104 | tf_op jit(solution)/shard_map/cond/branch_0_fun/ppermute | solution.py:367
  26.4 1.3 %collective-permute-start.9 = (bf16[768,256]{1,0:T(8,128)(2,1)S(1)}, bf16[768,256]{1,0:T(8,128)(2,1)S(1)}, u32[]{:S(2)}, u32[]{:S(2)}) collective-permute-start(bf16[768,256]{1,0:T(8,128)(2,1)S(1)} %get-tuple-element.31.b), channel_id=1, source_target_pairs={{0,8},{4,12},{9,1},{13,5},{18,26},{22,30},{27,19},{31,23}} | collective-permute-start | bytes 1179656 | tf_op jit(solution)/shard_map/cond/branch_0_fun/ppermute | solution.py:367
  27.7 0.7 collective-permute-start.8
  28.4 0.7 collective-permute-start.2
  29.1 1.9 %collective-permute-done.5.yb1 = bf16[512,256]{1,0:T(8,128)(2,1)S(1)} collective-permute-done((bf16[512,256]{1,0:T(8,128)(2,1)S(1)}, bf16[512,256]{1,0:T(8,128)(2,1)S(1)}, u32[]{:S(2)}, u32[]{:S(2)}) %collective-permute-start.5) | collective-permute-done | bytes 262176 | tf_op jit(solution)/shard_map/cond/branch_0_fun/ppermute | solution.py:367
  31.0 0.7 collective-permute-start.3
  31.7 0.7 collective-permute-start.7
  32.4 2.2 %collective-permute-done.9.xb = bf16[768,256]{1,0:T(8,128)(2,1)S(1)} collective-permute-done((bf16[768,256]{1,0:T(8,128)(2,1)S(1)}, bf16[768,256]{1,0:T(8,128)(2,1)S(1)}, u32[]{:S(2)}, u32[]{:S(2)}) %collective-permute-start.9) | collective-permute-done | bytes 393248 | tf_op jit(solution)/shard_map/cond/branch_0_fun/ppermute | solution.py:367
  34.7 0.4 branch_0_fun.34.own
  35.1 2.7 %branch_0_fun.37.left = bf16[512,3584]{1,0:T(8,128)(2,1)S(1)} custom-call(s32[7]{0:T(128)S(1)} %get-tuple-element.26.rows, s32[14]{0:T(128)S(1)} %get-tuple-element.28.cols, bf16[2304,4608]{1,0:T(8,128)(2,1)} %get-tuple-element.121.a), custom_call_target="tpu_custom_call" | custom-call | tf_op jit(solution)/shard_map/cond/branch_0_fun/pallas_call | solution.py:401
  37.8 2.7 %branch_0_fun.36.left = bf16[512,3584]{1,0:T(8,128)(2,1)S(1)} custom-call(s32[7]{0:T(128)S(1)} %get-tuple-element.26.rows, s32[14]{0:T(128)S(1)} %get-tuple-element.28.cols, bf16[2304,4608]{1,0:T(8,128)(2,1)} %get-tuple-element.121.a), custom_call_target="tpu_custom_call" | custom-call | tf_op jit(solution)/shard_map/cond/branch_0_fun/pallas_call | solution.py:401
  40.6 2.7 %branch_0_fun.35.left = bf16[512,3584]{1,0:T(8,128)(2,1)S(1)} custom-call(s32[7]{0:T(128)S(1)} %get-tuple-element.26.rows, s32[14]{0:T(128)S(1)} %get-tuple-element.28.cols, bf16[2304,4608]{1,0:T(8,128)(2,1)} %get-tuple-element.121.a), custom_call_target="tpu_custom_call" | custom-call | tf_op jit(solution)/shard_map/cond/branch_0_fun/pallas_call | solution.py:401
  43.3 0.8 branch_0_fun.38.own
  44.2 1.4 %branch_0_fun.39 = (f32[512,256]{1,0:T(8,128)S(1)}, s16[528,256]{1,0:T(8,128)(2,1)S(1)}, f32[256,256]{1,0:T(8,128)S(1)}) custom-call(bf16[512,3584]{1,0:T(8,128)(2,1)S(1)} %branch_0_fun.37.left, f32[512,256]{1,0:T(8,128)S(1)} %branch_0_fun.38.own, bf16[1792,256]{1,0:T(8,128)(2,1)S(1)} %collective-permute-done.10.other, ...), custom_call_target="tpu_custom_call" | custom-call | tf_op jit(solution)/shard_map/cond/branch_0_fun/pallas_call | solution.py:467
  45.6 5.4 %collective-permute-start.20 = (s16[528,256]{1,0:T(8,128)(2,1)S(1)}, s16[528,256]{1,0:T(8,128)(2,1)S(1)}, u32[]{:S(2)}, u32[]{:S(2)}) collective-permute-start(s16[528,256]{1,0:T(8,128)(2,1)S(1)} %get-tuple-element.46.mine), channel_id=1, source_target_pairs={{0,1},{3,2},{4,5},{7,6},{8,9},{11,10},{12,13},{15,14},{16,17},{19,... | collective-permute-start | bytes 811016 | tf_op jit(solution)/shard_map/cond/branch_0_fun/ppermute | solution.py:367
  51.0 1.9 %branch_0_fun.40 = (f32[512,256]{1,0:T(8,128)S(1)}, s16[528,256]{1,0:T(8,128)(2,1)S(1)}, f32[256,256]{1,0:T(8,128)S(1)}) custom-call(bf16[512,3584]{1,0:T(8,128)(2,1)S(1)} %branch_0_fun.36.left, bf16[1792,256]{1,0:T(8,128)(2,1)S(1)} %branch_0_fun.34.own, bf16[1792,256]{1,0:T(8,128)(2,1)S(1)} %collective-permute-done.10.other, ...), custom_call_target="tpu_custom_call" | custom-call | tf_op jit(solution)/shard_map/cond/branch_0_fun/pallas_call | solution.py:467
  52.9 1.3 %collective-permute-start.17 = (s16[528,256]{1,0:T(8,128)(2,1)S(1)}, s16[528,256]{1,0:T(8,128)(2,1)S(1)}, u32[]{:S(2)}, u32[]{:S(2)}) collective-permute-start(s16[528,256]{1,0:T(8,128)(2,1)S(1)} %get-tuple-element.44.mine), channel_id=1, source_target_pairs={{0,1},{3,2},{4,5},{7,6},{8,9},{11,10},{12,13},{15,14},{16,17},{19,... | collective-permute-start | bytes 811016 | tf_op jit(solution)/shard_map/cond/branch_0_fun/ppermute | solution.py:367
  54.2 1.9 %branch_0_fun.41 = (f32[512,256]{1,0:T(8,128)S(1)}, s16[528,256]{1,0:T(8,128)(2,1)S(1)}, f32[256,256]{1,0:T(8,128)S(1)}) custom-call(bf16[512,3584]{1,0:T(8,128)(2,1)S(1)} %branch_0_fun.35.left, bf16[1792,256]{1,0:T(8,128)(2,1)S(1)} %branch_0_fun.34.own, bf16[1792,256]{1,0:T(8,128)(2,1)S(1)} %collective-permute-done.10.other, ...), custom_call_target="tpu_custom_call" | custom-call | tf_op jit(solution)/shard_map/cond/branch_0_fun/pallas_call | solution.py:467
  56.1 1.3 %collective-permute-start.14 = (s16[528,256]{1,0:T(8,128)(2,1)S(1)}, s16[528,256]{1,0:T(8,128)(2,1)S(1)}, u32[]{:S(2)}, u32[]{:S(2)}) collective-permute-start(s16[528,256]{1,0:T(8,128)(2,1)S(1)} %get-tuple-element.42.mine), channel_id=1, source_target_pairs={{0,1},{3,2},{4,5},{7,6},{8,9},{11,10},{12,13},{15,14},{16,17},{19,... | collective-permute-start | bytes 811016 | tf_op jit(solution)/shard_map/cond/branch_0_fun/ppermute | solution.py:367
  57.4 2.1 %branch_0_fun.33.left = bf16[256,3584]{1,0:T(8,128)(2,1)S(1)} custom-call(s32[7]{0:T(128)S(1)} %get-tuple-element.26.rows, s32[14]{0:T(128)S(1)} %get-tuple-element.28.cols, bf16[2304,4608]{1,0:T(8,128)(2,1)} %get-tuple-element.121.a), custom_call_target="tpu_custom_call" | custom-call | tf_op jit(solution)/shard_map/cond/branch_0_fun/pallas_call | solution.py:401
  59.5 1.1 branch_0_fun.42
  60.7 0.5 collective-permute-start.23
  61.2 1.0 collective-permute-done.23.y
  62.3 0.2 branch_0_fun.49.mine
  62.5 0.7 collective-permute-start.21
  63.2 0.4 collective-permute-done.17.came
  63.6 0.2 branch_0_fun.47.mine
  63.9 0.7 collective-permute-start.18
  64.6 4.6 %collective-permute-done.14.came = s16[528,256]{1,0:T(8,128)(2,1)S(1)} collective-permute-done((s16[528,256]{1,0:T(8,128)(2,1)S(1)}, s16[528,256]{1,0:T(8,128)(2,1)S(1)}, u32[]{:S(2)}, u32[]{:S(2)}) %collective-permute-start.14) | collective-permute-done | bytes 270368 | tf_op jit(solution)/shard_map/cond/branch_0_fun/ppermute | solution.py:367
  69.1 0.2 branch_0_fun.45.mine
  69.4 0.7 collective-permute-start.15
  70.0 12.8 %collective-permute-start.11 = (s16[272,256]{1,0:T(8,128)(2,1)S(1)}, s16[272,256]{1,0:T(8,128)(2,1)S(1)}, u32[]{:S(2)}, u32[]{:S(2)}) collective-permute-start(s16[272,256]{1,0:T(8,128)(2,1)S(1)} %get-tuple-element.40.mine), channel_id=1, source_target_pairs={{0,1},{3,2},{4,5},{7,6},{8,9},{11,10},{12,13},{15,14},{16,17},{19,... | collective-permute-start | bytes 417800 | tf_op jit(solution)/shard_map/cond/branch_0_fun/ppermute | solution.py:367
  83.0 5.0 %collective-permute-done.25.y = f32[256,128]{1,0:T(8,128)S(1)} collective-permute-done((f32[256,128]{1,0:T(8,128)S(1)}, f32[256,128]{1,0:T(8,128)S(1)}, u32[]{:S(2)}, u32[]{:S(2)}) %collective-permute-start.25) | collective-permute-done | bytes 131104 | tf_op jit(solution)/shard_map/cond/branch_0_fun/ppermute | solution.py:367
  88.1 1.6 %collective-permute-start.26 = (s16[272,128]{1,0:T(8,128)(2,1)S(1)}, s16[272,128]{1,0:T(8,128)(2,1)S(1)}, u32[]{:S(2)}, u32[]{:S(2)}) collective-permute-start(s16[272,128]{1,0:T(8,128)(2,1)S(1)} %branch_0_fun.59.mine), channel_id=1, source_target_pairs={{0,1},{3,2},{4,5},{7,6},{8,9},{11,10},{12,13},{15,14},{16,17},{19,... | collective-permute-start | bytes 208904 | tf_op jit(solution)/shard_map/cond/branch_0_fun/ppermute | solution.py:367
  89.7 0.1 branch_0_fun.43.mine
  89.9 0.7 collective-permute-start.12
  90.6 0.3 branch_0_fun.50.total
  90.9 1.3 %collective-permute-start.22 = (s16[528,256]{1,0:T(8,128)(2,1)S(1)}, s16[528,256]{1,0:T(8,128)(2,1)S(1)}, u32[]{:S(2)}, u32[]{:S(2)}) collective-permute-start(s16[528,256]{1,0:T(8,128)(2,1)S(1)} %branch_0_fun.50.total), channel_id=1, source_target_pairs={{1,0},{2,3},{5,4},{6,7},{9,8},{10,11},{13,12},{14,15},{17,16},{18,... | collective-permute-start | bytes 811016 | tf_op jit(solution)/shard_map/cond/branch_0_fun/ppermute | solution.py:367
  92.2 0.3 branch_0_fun.48.total
  92.6 1.3 %collective-permute-start.19 = (s16[528,256]{1,0:T(8,128)(2,1)S(1)}, s16[528,256]{1,0:T(8,128)(2,1)S(1)}, u32[]{:S(2)}, u32[]{:S(2)}) collective-permute-start(s16[528,256]{1,0:T(8,128)(2,1)S(1)} %branch_0_fun.48.total), channel_id=1, source_target_pairs={{1,0},{2,3},{5,4},{6,7},{9,8},{10,11},{13,12},{14,15},{17,16},{18,... | collective-permute-start | bytes 811016 | tf_op jit(solution)/shard_map/cond/branch_0_fun/ppermute | solution.py:367
  93.9 0.3 branch_0_fun.46.total
  94.2 1.3 %collective-permute-start.16 = (s16[528,256]{1,0:T(8,128)(2,1)S(1)}, s16[528,256]{1,0:T(8,128)(2,1)S(1)}, u32[]{:S(2)}, u32[]{:S(2)}) collective-permute-start(s16[528,256]{1,0:T(8,128)(2,1)S(1)} %branch_0_fun.46.total), channel_id=1, source_target_pairs={{1,0},{2,3},{5,4},{6,7},{9,8},{10,11},{13,12},{14,15},{17,16},{18,... | collective-permute-start | bytes 811016 | tf_op jit(solution)/shard_map/cond/branch_0_fun/ppermute | solution.py:367
  95.5 0.1 branch_0_fun.60.mine
  95.7 0.7 collective-permute-start.27
  96.3 0.2 branch_0_fun.61.total
  96.5 1.3 %collective-permute-start.28 = (s16[272,128]{1,0:T(8,128)(2,1)S(1)}, s16[272,128]{1,0:T(8,128)(2,1)S(1)}, u32[]{:S(2)}, u32[]{:S(2)}) collective-permute-start(s16[272,128]{1,0:T(8,128)(2,1)S(1)} %branch_0_fun.61.total), channel_id=1, source_target_pairs={{1,0},{2,3},{5,4},{6,7},{9,8},{10,11},{13,12},{14,15},{17,16},{18,... | collective-permute-start | bytes 208904 | tf_op jit(solution)/shard_map/cond/branch_0_fun/ppermute | solution.py:367
  97.8 0.2 branch_0_fun.44.total
  98.0 1.3 %collective-permute-start.13 = (s16[272,256]{1,0:T(8,128)(2,1)S(1)}, s16[272,256]{1,0:T(8,128)(2,1)S(1)}, u32[]{:S(2)}, u32[]{:S(2)}) collective-permute-start(s16[272,256]{1,0:T(8,128)(2,1)S(1)} %branch_0_fun.44.total), channel_id=1, source_target_pairs={{1,0},{2,3},{5,4},{6,7},{9,8},{10,11},{13,12},{14,15},{17,16},{18,... | collective-permute-start | bytes 417800 | tf_op jit(solution)/shard_map/cond/branch_0_fun/ppermute | solution.py:367
  99.3 15.2 %collective-permute-done.28.came = s16[272,128]{1,0:T(8,128)(2,1)S(1)} collective-permute-done((s16[272,128]{1,0:T(8,128)(2,1)S(1)}, s16[272,128]{1,0:T(8,128)(2,1)S(1)}, u32[]{:S(2)}, u32[]{:S(2)}) %collective-permute-start.28) | collective-permute-done | bytes 69664 | tf_op jit(solution)/shard_map/cond/branch_0_fun/ppermute | solution.py:367
  114.6 1.2 %collective-permute-done.29.other = s16[272,128]{1,0:T(8,128)(2,1)S(1)} collective-permute-done((s16[272,128]{1,0:T(8,128)(2,1)S(1)}, s16[272,128]{1,0:T(8,128)(2,1)S(1)}, u32[]{:S(2)}, u32[]{:S(2)}) %collective-permute-start.29) | collective-permute-done | bytes 69664 | tf_op jit(solution)/shard_map/cond/branch_0_fun/ppermute | solution.py:367
  115.9 0.8 branch_0_fun.63
  116.6 1.1 branch_0_fun.51.refs_0_
  117.7 0.9 branch_0_fun.52.refs_0_
  118.7 0.9 branch_0_fun.53.refs_0_
  119.6 0.8 branch_0_fun.54
  120.4 1.4 %copy-done = f32[2304,256]{1,0:T(8,128)} copy-done((f32[2304,256]{1,0:T(8,128)}, f32[2304,256]{1,0:T(8,128)S(1)}, u32[]{:S(2)}) %copy-start) | copy-done | bytes 2359320 | tf_op jit(solution)/shard_map/cond
  (36 shorter events, 0.6 us)
Async XLA Ops:
  5.3 22.4 %collective-permute-start = (bf16[512,256]{1,0:T(8,128)(2,1)S(1)}, bf16[512,256]{1,0:T(8,128)(2,1)S(1)}, u32[]{:S(2)}, u32[]{:S(2)}) collective-permute-start(bf16[512,256]{1,0:T(8,128)(2,1)S(1)} %get-tuple-element.32), channel_id=1, source_target_pairs={{0,8},{4,12},{9,1},{13,5},{18,26},{22,30},{27,19},{31,23}} | collective-permute-start | bytes 786440 | tf_op jit(solution)/shard_map/cond/branch_0_fun/ppermute | solution.py:367
  10.0 24.6 %collective-permute-start.4 = (bf16[1024,256]{1,0:T(8,128)(2,1)S(1)}, bf16[1024,256]{1,0:T(8,128)(2,1)S(1)}, u32[]{:S(2)}, u32[]{:S(2)}) collective-permute-start(bf16[1024,256]{1,0:T(8,128)(2,1)S(1)} %get-tuple-element.30.a), channel_id=1, source_target_pairs={{0,16},{4,20},{9,25},{13,29},{18,2},{22,6},{27,11},{31,15}} | collective-permute-start | bytes 1572872 | tf_op jit(solution)/shard_map/cond/branch_0_fun/ppermute | solution.py:367
  11.3 15.1 %collective-permute-start.6 = (bf16[256,256]{1,0:T(8,128)(2,1)S(1)}, bf16[256,256]{1,0:T(8,128)(2,1)S(1)}, u32[]{:S(2)}, u32[]{:S(2)}) collective-permute-start(bf16[256,256]{1,0:T(8,128)(2,1)S(1)} %get-tuple-element.35), channel_id=1, source_target_pairs={{0,16},{4,20},{9,25},{13,29},{18,2},{22,6},{27,11},{31,15}} | collective-permute-start | bytes 393224 | tf_op jit(solution)/shard_map/cond/branch_0_fun/ppermute | solution.py:367
  12.6 15.8 %collective-permute-start.1 = (bf16[512,256]{1,0:T(8,128)(2,1)S(1)}, bf16[512,256]{1,0:T(8,128)(2,1)S(1)}, u32[]{:S(2)}, u32[]{:S(2)}) collective-permute-start(bf16[512,256]{1,0:T(8,128)(2,1)S(1)} %get-tuple-element.33), channel_id=1, source_target_pairs={{0,8},{4,12},{9,1},{13,5},{18,26},{22,30},{27,19},{31,23}} | collective-permute-start | bytes 786440 | tf_op jit(solution)/shard_map/cond/branch_0_fun/ppermute | solution.py:367
  14.0 17.1 %collective-permute-start.5 = (bf16[512,256]{1,0:T(8,128)(2,1)S(1)}, bf16[512,256]{1,0:T(8,128)(2,1)S(1)}, u32[]{:S(2)}, u32[]{:S(2)}) collective-permute-start(bf16[512,256]{1,0:T(8,128)(2,1)S(1)} %get-tuple-element.34), channel_id=1, source_target_pairs={{0,16},{4,20},{9,25},{13,29},{18,2},{22,6},{27,11},{31,15}} | collective-permute-start | bytes 786440 | tf_op jit(solution)/shard_map/cond/branch_0_fun/ppermute | solution.py:367
  26.4 8.2 %collective-permute-start.9 = (bf16[768,256]{1,0:T(8,128)(2,1)S(1)}, bf16[768,256]{1,0:T(8,128)(2,1)S(1)}, u32[]{:S(2)}, u32[]{:S(2)}) collective-permute-start(bf16[768,256]{1,0:T(8,128)(2,1)S(1)} %get-tuple-element.31.b), channel_id=1, source_target_pairs={{0,8},{4,12},{9,1},{13,5},{18,26},{22,30},{27,19},{31,23}} | collective-permute-start | bytes 1179656 | tf_op jit(solution)/shard_map/cond/branch_0_fun/ppermute | solution.py:367
  27.7 4.0 %collective-permute-start.8 = (bf16[256,256]{1,0:T(8,128)(2,1)S(1)}, bf16[256,256]{1,0:T(8,128)(2,1)S(1)}, u32[]{:S(2)}, u32[]{:S(2)}) collective-permute-start(bf16[256,256]{1,0:T(8,128)(2,1)S(1)} %collective-permute-done.6.yb2), channel_id=1, source_target_pairs={{2,10},{6,14},{11,3},{15,7},{16,24},{20,28},{25,17},{29,21}} | collective-permute-start | bytes 393224 | tf_op jit(solution)/shard_map/cond/branch_0_fun/ppermute | solution.py:367
  28.4 6.2 %collective-permute-start.2 = (bf16[512,256]{1,0:T(8,128)(2,1)S(1)}, bf16[512,256]{1,0:T(8,128)(2,1)S(1)}, u32[]{:S(2)}, u32[]{:S(2)}) collective-permute-start(bf16[512,256]{1,0:T(8,128)(2,1)S(1)} %collective-permute-done.xa1), channel_id=1, source_target_pairs={{1,17},{5,21},{8,24},{12,28},{19,3},{23,7},{26,10},{30,14}} | collective-permute-start | bytes 786440 | tf_op jit(solution)/shard_map/cond/branch_0_fun/ppermute | solution.py:367
  31.0 3.6 %collective-permute-start.3 = (bf16[512,256]{1,0:T(8,128)(2,1)S(1)}, bf16[512,256]{1,0:T(8,128)(2,1)S(1)}, u32[]{:S(2)}, u32[]{:S(2)}) collective-permute-start(bf16[512,256]{1,0:T(8,128)(2,1)S(1)} %collective-permute-done.1.xa2), channel_id=1, source_target_pairs={{1,17},{5,21},{8,24},{12,28},{19,3},{23,7},{26,10},{30,14}} | collective-permute-start | bytes 786440 | tf_op jit(solution)/shard_map/cond/branch_0_fun/ppermute | solution.py:367
  31.7 2.9 %collective-permute-start.7 = (bf16[512,256]{1,0:T(8,128)(2,1)S(1)}, bf16[512,256]{1,0:T(8,128)(2,1)S(1)}, u32[]{:S(2)}, u32[]{:S(2)}) collective-permute-start(bf16[512,256]{1,0:T(8,128)(2,1)S(1)} %collective-permute-done.5.yb1), channel_id=1, source_target_pairs={{2,10},{6,14},{11,3},{15,7},{16,24},{20,28},{25,17},{29,21}} | collective-permute-start | bytes 786440 | tf_op jit(solution)/shard_map/cond/branch_0_fun/ppermute | solution.py:367
  35.0 9.1 %collective-permute-start.10 = (bf16[1792,256]{1,0:T(8,128)(2,1)S(1)}, bf16[1792,256]{1,0:T(8,128)(2,1)S(1)}, u32[]{:S(2)}, u32[]{:S(2)}) collective-permute-start(bf16[1792,256]{1,0:T(8,128)(2,1)S(1)} %branch_0_fun.34.own), channel_id=1, source_target_pairs={{0,4},{1,5},{2,6},{3,7},{4,0},{5,1},{6,2},{7,3},{8,12},{9,13},{10,... | collective-permute-start | bytes 2752520 | tf_op jit(solution)/shard_map/cond/branch_0_fun/ppermute | solution.py:367
  45.6 16.7 %collective-permute-start.20 = (s16[528,256]{1,0:T(8,128)(2,1)S(1)}, s16[528,256]{1,0:T(8,128)(2,1)S(1)}, u32[]{:S(2)}, u32[]{:S(2)}) collective-permute-start(s16[528,256]{1,0:T(8,128)(2,1)S(1)} %get-tuple-element.46.mine), channel_id=1, source_target_pairs={{0,1},{3,2},{4,5},{7,6},{8,9},{11,10},{12,13},{15,14},{16,17},{19,... | collective-permute-start | bytes 811016 | tf_op jit(solution)/shard_map/cond/branch_0_fun/ppermute | solution.py:367
  52.9 10.7 %collective-permute-start.17 = (s16[528,256]{1,0:T(8,128)(2,1)S(1)}, s16[528,256]{1,0:T(8,128)(2,1)S(1)}, u32[]{:S(2)}, u32[]{:S(2)}) collective-permute-start(s16[528,256]{1,0:T(8,128)(2,1)S(1)} %get-tuple-element.44.mine), channel_id=1, source_target_pairs={{0,1},{3,2},{4,5},{7,6},{8,9},{11,10},{12,13},{15,14},{16,17},{19,... | collective-permute-start | bytes 811016 | tf_op jit(solution)/shard_map/cond/branch_0_fun/ppermute | solution.py:367
  56.1 13.0 %collective-permute-start.14 = (s16[528,256]{1,0:T(8,128)(2,1)S(1)}, s16[528,256]{1,0:T(8,128)(2,1)S(1)}, u32[]{:S(2)}, u32[]{:S(2)}) collective-permute-start(s16[528,256]{1,0:T(8,128)(2,1)S(1)} %get-tuple-element.42.mine), channel_id=1, source_target_pairs={{0,1},{3,2},{4,5},{7,6},{8,9},{11,10},{12,13},{15,14},{16,17},{19,... | collective-permute-start | bytes 811016 | tf_op jit(solution)/shard_map/cond/branch_0_fun/ppermute | solution.py:367
  60.7 1.4 %collective-permute-start.23 = (f32[256,128]{1,0:T(8,128)S(1)}, f32[256,128]{1,0:T(8,128)S(1)}, u32[]{:S(2)}, u32[]{:S(2)}) collective-permute-start(f32[256,128]{1,0:T(8,128)S(1)} %get-tuple-element.50), channel_id=1, source_target_pairs={{0,4},{1,5},{2,6},{3,7},{4,0},{5,1},{6,2},{7,3},{8,12},{9,13},{10,... | collective-permute-start | bytes 393224 | tf_op jit(solution)/shard_map/cond/branch_0_fun/ppermute | solution.py:367
  62.2 20.7 %collective-permute-start.24 = (f32[256,128]{1,0:T(8,128)S(1)}, f32[256,128]{1,0:T(8,128)S(1)}, u32[]{:S(2)}, u32[]{:S(2)}) collective-permute-start(f32[256,128]{1,0:T(8,128)S(1)} %branch_0_fun.56.x), channel_id=1, source_target_pairs={{0,8},{1,9},{2,10},{3,11},{4,12},{5,13},{6,14},{7,15},{8,0},{9,1},... | collective-permute-start | bytes 393224 | tf_op jit(solution)/shard_map/cond/branch_0_fun/ppermute | solution.py:367
  62.5 28.0 %collective-permute-start.21 = (s16[528,256]{1,0:T(8,128)(2,1)S(1)}, s16[528,256]{1,0:T(8,128)(2,1)S(1)}, u32[]{:S(2)}, u32[]{:S(2)}) collective-permute-start(s16[528,256]{1,0:T(8,128)(2,1)S(1)} %branch_0_fun.49.mine), channel_id=1, source_target_pairs={{1,2},{2,1},{5,6},{6,5},{9,10},{10,9},{13,14},{14,13},{17,18},{18,... | collective-permute-start | bytes 811016 | tf_op jit(solution)/shard_map/cond/branch_0_fun/ppermute | solution.py:367
  63.9 28.3 %collective-permute-start.18 = (s16[528,256]{1,0:T(8,128)(2,1)S(1)}, s16[528,256]{1,0:T(8,128)(2,1)S(1)}, u32[]{:S(2)}, u32[]{:S(2)}) collective-permute-start(s16[528,256]{1,0:T(8,128)(2,1)S(1)} %branch_0_fun.47.mine), channel_id=1, source_target_pairs={{1,2},{2,1},{5,6},{6,5},{9,10},{10,9},{13,14},{14,13},{17,18},{18,... | collective-permute-start | bytes 811016 | tf_op jit(solution)/shard_map/cond/branch_0_fun/ppermute | solution.py:367
  69.4 24.5 %collective-permute-start.15 = (s16[528,256]{1,0:T(8,128)(2,1)S(1)}, s16[528,256]{1,0:T(8,128)(2,1)S(1)}, u32[]{:S(2)}, u32[]{:S(2)}) collective-permute-start(s16[528,256]{1,0:T(8,128)(2,1)S(1)} %branch_0_fun.45.mine), channel_id=1, source_target_pairs={{1,2},{2,1},{5,6},{6,5},{9,10},{10,9},{13,14},{14,13},{17,18},{18,... | collective-permute-start | bytes 811016 | tf_op jit(solution)/shard_map/cond/branch_0_fun/ppermute | solution.py:367
  70.0 19.7 %collective-permute-start.11 = (s16[272,256]{1,0:T(8,128)(2,1)S(1)}, s16[272,256]{1,0:T(8,128)(2,1)S(1)}, u32[]{:S(2)}, u32[]{:S(2)}) collective-permute-start(s16[272,256]{1,0:T(8,128)(2,1)S(1)} %get-tuple-element.40.mine), channel_id=1, source_target_pairs={{0,1},{3,2},{4,5},{7,6},{8,9},{11,10},{12,13},{15,14},{16,17},{19,... | collective-permute-start | bytes 417800 | tf_op jit(solution)/shard_map/cond/branch_0_fun/ppermute | solution.py:367
  82.9 33.0 %copy-start.3 = (f32[256,256]{1,0:T(8,128)S(1)}, f32[256,256]{1,0:T(8,128)}, u32[]{:S(2)}) copy-start(f32[256,256]{1,0:T(8,128)} %get-tuple-element.124.base) | copy-start | bytes 786436 | tf_op jit(solution)/shard_map/cond
  82.9 5.1 %collective-permute-start.25 = (f32[256,128]{1,0:T(8,128)S(1)}, f32[256,128]{1,0:T(8,128)S(1)}, u32[]{:S(2)}, u32[]{:S(2)}) collective-permute-start(f32[256,128]{1,0:T(8,128)S(1)} %branch_0_fun.57.x), channel_id=1, source_target_pairs={{0,16},{1,17},{2,18},{3,19},{4,20},{5,21},{6,22},{7,23},{8,24},{9,... | collective-permute-start | bytes 393224 | tf_op jit(solution)/shard_map/cond/branch_0_fun/ppermute | solution.py:367
  88.1 7.4 %collective-permute-start.26 = (s16[272,128]{1,0:T(8,128)(2,1)S(1)}, s16[272,128]{1,0:T(8,128)(2,1)S(1)}, u32[]{:S(2)}, u32[]{:S(2)}) collective-permute-start(s16[272,128]{1,0:T(8,128)(2,1)S(1)} %branch_0_fun.59.mine), channel_id=1, source_target_pairs={{0,1},{3,2},{4,5},{7,6},{8,9},{11,10},{12,13},{15,14},{16,17},{19,... | collective-permute-start | bytes 208904 | tf_op jit(solution)/shard_map/cond/branch_0_fun/ppermute | solution.py:367
  89.7 26.9 %copy-start.6 = (s32[72]{0:T(128)S(1)}, s32[72]{0:T(128)}, u32[]{:S(2)}) copy-start(s32[72]{0:T(128)} %get-tuple-element.24.live) | copy-start | bytes 868 | tf_op jit(solution)/shard_map/cond
  89.9 7.9 %collective-permute-start.12 = (s16[272,256]{1,0:T(8,128)(2,1)S(1)}, s16[272,256]{1,0:T(8,128)(2,1)S(1)}, u32[]{:S(2)}, u32[]{:S(2)}) collective-permute-start(s16[272,256]{1,0:T(8,128)(2,1)S(1)} %branch_0_fun.43.mine), channel_id=1, source_target_pairs={{1,2},{2,1},{5,6},{6,5},{9,10},{10,9},{13,14},{14,13},{17,18},{18,... | collective-permute-start | bytes 417800 | tf_op jit(solution)/shard_map/cond/branch_0_fun/ppermute | solution.py:367
  90.9 25.7 %collective-permute-start.22 = (s16[528,256]{1,0:T(8,128)(2,1)S(1)}, s16[528,256]{1,0:T(8,128)(2,1)S(1)}, u32[]{:S(2)}, u32[]{:S(2)}) collective-permute-start(s16[528,256]{1,0:T(8,128)(2,1)S(1)} %branch_0_fun.50.total), channel_id=1, source_target_pairs={{1,0},{2,3},{5,4},{6,7},{9,8},{10,11},{13,12},{14,15},{17,16},{18,... | collective-permute-start | bytes 811016 | tf_op jit(solution)/shard_map/cond/branch_0_fun/ppermute | solution.py:367
  92.6 25.2 %collective-permute-start.19 = (s16[528,256]{1,0:T(8,128)(2,1)S(1)}, s16[528,256]{1,0:T(8,128)(2,1)S(1)}, u32[]{:S(2)}, u32[]{:S(2)}) collective-permute-start(s16[528,256]{1,0:T(8,128)(2,1)S(1)} %branch_0_fun.48.total), channel_id=1, source_target_pairs={{1,0},{2,3},{5,4},{6,7},{9,8},{10,11},{13,12},{14,15},{17,16},{18,... | collective-permute-start | bytes 811016 | tf_op jit(solution)/shard_map/cond/branch_0_fun/ppermute | solution.py:367
  94.2 24.5 %collective-permute-start.16 = (s16[528,256]{1,0:T(8,128)(2,1)S(1)}, s16[528,256]{1,0:T(8,128)(2,1)S(1)}, u32[]{:S(2)}, u32[]{:S(2)}) collective-permute-start(s16[528,256]{1,0:T(8,128)(2,1)S(1)} %branch_0_fun.46.total), channel_id=1, source_target_pairs={{1,0},{2,3},{5,4},{6,7},{9,8},{10,11},{13,12},{14,15},{17,16},{18,... | collective-permute-start | bytes 811016 | tf_op jit(solution)/shard_map/cond/branch_0_fun/ppermute | solution.py:367
  95.7 0.7 collective-permute-start.27
  96.5 18.0 %collective-permute-start.28 = (s16[272,128]{1,0:T(8,128)(2,1)S(1)}, s16[272,128]{1,0:T(8,128)(2,1)S(1)}, u32[]{:S(2)}, u32[]{:S(2)}) collective-permute-start(s16[272,128]{1,0:T(8,128)(2,1)S(1)} %branch_0_fun.61.total), channel_id=1, source_target_pairs={{1,0},{2,3},{5,4},{6,7},{9,8},{10,11},{13,12},{14,15},{17,16},{18,... | collective-permute-start | bytes 208904 | tf_op jit(solution)/shard_map/cond/branch_0_fun/ppermute | solution.py:367
  98.0 21.6 %collective-permute-start.13 = (s16[272,256]{1,0:T(8,128)(2,1)S(1)}, s16[272,256]{1,0:T(8,128)(2,1)S(1)}, u32[]{:S(2)}, u32[]{:S(2)}) collective-permute-start(s16[272,256]{1,0:T(8,128)(2,1)S(1)} %branch_0_fun.44.total), channel_id=1, source_target_pairs={{1,0},{2,3},{5,4},{6,7},{9,8},{10,11},{13,12},{14,15},{17,16},{18,... | collective-permute-start | bytes 417800 | tf_op jit(solution)/shard_map/cond/branch_0_fun/ppermute | solution.py:367
  114.5 1.3 %collective-permute-start.29 = (s16[272,128]{1,0:T(8,128)(2,1)S(1)}, s16[272,128]{1,0:T(8,128)(2,1)S(1)}, u32[]{:S(2)}, u32[]{:S(2)}) collective-permute-start(s16[272,128]{1,0:T(8,128)(2,1)S(1)} %branch_0_fun.62.mine), channel_id=1, source_target_pairs={{0,4},{1,5},{2,6},{3,7},{4,0},{5,1},{6,2},{7,3},{8,12},{9,13},{10,... | collective-permute-start | bytes 208904 | tf_op jit(solution)/shard_map/cond/branch_0_fun/ppermute | solution.py:367
  120.4 1.4 %copy-start = (f32[2304,256]{1,0:T(8,128)}, f32[2304,256]{1,0:T(8,128)S(1)}, u32[]{:S(2)}) copy-start(f32[2304,256]{1,0:T(8,128)S(1)} %branch_0_fun.54) | copy-start | bytes 7077892 | tf_op jit(solution)/shard_map/cond
